TPU v7x, 128 devices: a whole 4x4x4 slice. The times are simulated.
128 devices in a mesh: dev: 128 (over y, z, x, core).
Axes of the slice: x: 4, y: 4, z: 4, core: 2. Of those that a mesh axis runs over, the one named last changes fastest.
Arguments:
- micrographs: bfloat16 [512, 1024, 1024], P('dev'), may hold values from -32 to 32
- positions: int32 [2, 512, 64], P(None, 'dev'), may hold values from 0 to 960
- counts: int32 [512], P('dev'), may hold values from 0 to 64, as said below
- dest_rows: int32 [512, 64], P('dev'), may hold values from -1 to 16383, as said below
- templates: bfloat16 [100, 32, 128], replicated, may hold values from -1 to 1
Outputs:
- class_means: float32 [100, 32, 128], replicated
- loglik: float32 [16384], P('dev')
Inputs may be any that keep to these rules, and one draw needn't show every extreme that they name: All counts sum to 16384; the counts of one device sum to at most 256, and some device's counts reach it. `dest_rows`: slot j of micrograph i holds -1 when j >= counts[i], else a row; every row of 0 to 16383 occurs once over all devices. The rows held by one device fall at most 2 times into the rows d * 128 to (d + 1) * 128 - 1 of any one device d, and some device reaches 2 with every device.
All inputs are finite; a program needn't handle non-finite values.
Results may differ from a plain program's by a relative error of at most 0.0055.
The roundings to bfloat16 on the way count: a program that leaves them out, or rounds other values in their place, can miss the bound.
Values may be sent and summed in bfloat16 or wider, within the bound.
A program may use at most 192 MiB of HBM per device.

v0:
```python
import functools
import numpy as np
import jax
import jax.numpy as jnp
from jax import lax
from jax.experimental import pallas as pl
from jax.experimental.pallas import tpu as pltpu

BOX = 64
RAD = 32
ANG = 128
CLASSES = 100
ROTS = 36
CPAD = 104
QROT = 4
BASE = 9
NROWS = 4 * 2 * CPAD + 112
F32 = jnp.float32
BF16 = jnp.bfloat16


def sample_points():
    center = np.float32((BOX - 1) / 2.0)
    radius = (np.arange(RAD, dtype=np.float32) + np.float32(0.5)) * np.float32(BOX / 2.0 - 1.0) / np.float32(RAD)
    theta = np.float32(2.0 * np.pi) * np.arange(ANG, dtype=np.float32) / np.float32(ANG)
    ys = (center + radius[:, None] * np.sin(theta)[None, :]).reshape(1, -1)
    xs = (center + radius[:, None] * np.cos(theta)[None, :]).reshape(1, -1)
    return ys.astype(np.float32), xs.astype(np.float32)


def rotation_taps():
    a = np.arange(ANG, dtype=np.float32)
    taps = []
    for k in range(BASE):
        shift = np.float32(k) * np.float32(ANG) / np.float32(ROTS)
        d = a - np.float32(0) - shift
        d = d - ANG * np.floor(d / np.float32(ANG) + np.float32(0.5))
        w = np.maximum(np.float32(0), np.float32(1) - np.abs(d)).astype(jnp.bfloat16).astype(np.float32)
        first = int(32 * k // 9)
        taps.append((first, float(w[first]), float(w[(first + 1) % ANG]) if k else 0.0))
    return taps


TAPS = rotation_taps()


def local_kernel(pos, counts, mic, dest, ys, xs, tmpl, g_out, tot_out, ll_out,
                 raw, planes, flat, boxes, wtile, tflat, rot, esum, shifted, scores, weights, tsum, sems):
    mics = mic.shape[0]
    slots = pos.shape[2]
    parts = mics * slots

    def fetch(i):
        return pltpu.make_async_copy(mic.at[i], raw.at[i % 2], sems.at[i % 2])

    fetch(0).start()
    fetch(1).start()

    lane1 = lax.broadcasted_iota(jnp.int32, (1, ANG), 1)

    tflat[pl.ds(CLASSES * RAD, (CPAD - CLASSES) * RAD), :] = jnp.zeros(((CPAD - CLASSES) * RAD, ANG), F32)
    tflat[pl.ds(0, CLASSES * RAD), :] = tmpl[...].reshape(CLASSES * RAD, ANG).astype(F32)
    esum[...] = jnp.zeros_like(esum)
    rot[pl.ds(8 * CPAD, 112), :] = jnp.zeros((112, RAD * ANG), BF16)

    def rotate_radius(r, _):
        x = tflat[pl.ds(r, CPAD, stride=RAD), :]
        x1 = pltpu.roll(x, 1, 1)
        col = pl.ds(pl.multiple_of(r * ANG, ANG), ANG)
        turned = []
        for first, w0, w1 in TAPS:
            y = x if w1 == 0.0 else w0 * x + w1 * x1
            turned.append(pltpu.roll(y, first, 1) if first else y)
        turned.append(jnp.zeros((8, ANG), F32))
        for i in range(0, BASE, 2):
            pair = jnp.concatenate(turned[i : i + 2], axis=0).astype(BF16)
            rot[pl.ds(i * CPAD, pair.shape[0]), col] = pair
            wide = pair.astype(F32)
            esum[pl.ds(i * CPAD, pair.shape[0]), :] += wide * wide
        return 0

    lax.fori_loop(0, RAD, rotate_radius, 0)

    lanes = lax.broadcasted_iota(jnp.int32, (BOX // 2, ANG), 1)
    for i in range(mics):
        fetch(i).wait()
        for t in range(8):
            planes[t, :, :] = raw[i % 2, :, t * ANG : (t + 1) * ANG].astype(F32)
        if i + 2 < mics:
            fetch(i + 2).start()

        def cut(j, _, i=i):
            y = pos[0, i, j]
            x = pos[1, i, j]
            t = x // ANG
            s = x - t * ANG
            t1 = jnp.minimum(t + 1, 7)
            even = pl.ds(y, BOX // 2, stride=2)
            odd = pl.ds(y + 1, BOX // 2, stride=2)
            keep = lanes >= s
            e = jnp.where(keep, planes[t, even, :], planes[t1, even, :])
            o = jnp.where(keep, planes[t, odd, :], planes[t1, odd, :])
            e = pltpu.roll(e, lax.rem(ANG - s, ANG), 1)
            o = pltpu.roll(o, lax.rem(ANG + BOX - s, ANG), 1)
            flat[pl.ds(i * slots + j, BOX // 2, stride=parts), :] = jnp.where(lanes < BOX, e, o)
            return 0

        lax.fori_loop(0, slots, cut, 0, unroll=4)

    for s in range(BOX // 2):
        boxes[:, s * ANG : (s + 1) * ANG] = flat[pl.ds(s * parts, parts), :].astype(BF16)

    pix = lax.broadcasted_iota(jnp.int32, (BOX, 2 * ANG), 0).astype(F32)
    for g in range(RAD // 2):
        radius = (2 * g + 1.5) * (BOX / 2.0 - 1.0) / RAD
        low = int(np.floor(31.5 - radius)) - 1
        low = max(0, low // 4 * 4)
        high = BOX - low
        cols = slice(g * 2 * ANG, (g + 1) * 2 * ANG)
        rw = jnp.maximum(0.0, 1.0 - jnp.abs(pix - ys[:, cols]))
        cw = jnp.maximum(0.0, 1.0 - jnp.abs(pix - xs[:, cols]))
        w = wtile.at[g % 2]
        for u in range(low, high):
            w[u * BOX : (u + 1) * BOX, :] = (rw[u : u + 1, :] * cw).astype(BF16)
        p = jnp.dot(boxes[:, low * BOX : high * BOX], w[low * BOX : high * BOX, :], preferred_element_type=F32)
        for h in range(2):
            half = p[:, h * ANG : (h + 1) * ANG]
            c0 = (2 * g + h) * ANG
            for j in range(QROT):
                part = half if j == 0 else pltpu.roll(half, ANG - 32 * j, 1)
                shifted[j * parts : (j + 1) * parts, c0 : c0 + ANG] = part.astype(BF16)

    rows = lax.broadcasted_iota(jnp.int32, (NROWS, 1), 0)
    energy = 0.5 * jnp.sum(esum[...], axis=1, keepdims=True)
    pad = (lax.rem(rows, CPAD) >= CLASSES) | (rows >= BASE * CPAD)
    energy = jnp.where(pad, 1e30, energy)

    def score(j, peak):
        rows_j = pl.ds(pl.multiple_of(j * parts, parts), parts)
        prod = lax.dot_general(rot[...], shifted[rows_j, :], (((1,), (1,)), ((), ())), preferred_element_type=F32)
        prod = prod - energy
        scores[:, rows_j] = prod
        return jnp.maximum(peak, jnp.max(prod, axis=0, keepdims=True))

    peak = lax.fori_loop(0, QROT, score, jnp.full((1, parts), -3e38, F32))
    peak4 = jnp.concatenate([peak] * QROT, axis=1)

    def expo(n, acc):
        rr = pl.ds(pl.multiple_of(n * 16, 16), 16)
        e = jnp.exp(scores[rr, :] - peak4)
        scores[rr, :] = e
        return acc + e[:8] + e[8:]

    acc = lax.fori_loop(0, NROWS // 16, expo, jnp.zeros((8, QROT * parts), F32))
    norm = jnp.sum(acc, axis=0, keepdims=True)
    norm = sum(norm[:, j * parts : (j + 1) * parts] for j in range(QROT))
    loglik = peak + jnp.log(norm)

    lane = lax.broadcasted_iota(jnp.int32, (1, parts), 1)
    target = dest[...]
    live = target >= 0
    for i in range(mics):
        live = live & ((lane < i * slots + counts[i]) | (lane >= (i + 1) * slots))
    inv = jnp.where(live, 1.0 / norm, 0.0)
    inv4 = jnp.concatenate([inv] * QROT, axis=1)

    def weigh(n, _):
        rr = pl.ds(pl.multiple_of(n * 16, 16), 16)
        w = (scores[rr, :] * inv4).astype(BF16)
        weights[rr, :] = w
        wide = w.astype(F32)
        tsum[rr, :] = sum(wide[:, k * ANG : (k + 1) * ANG] for k in range(QROT * parts // ANG))
        return 0

    lax.fori_loop(0, NROWS // 16, weigh, 0)
    tot = jnp.sum(tsum[...], axis=1, keepdims=True)
    tot = sum(tot[i * CPAD : (i + 1) * CPAD] for i in range(BASE))
    spot = lax.broadcasted_iota(jnp.int32, (CPAD, ANG), 0) == lax.broadcasted_iota(jnp.int32, (CPAD, ANG), 1)
    tot_out[...] = jnp.sum(jnp.where(spot, tot, 0.0), axis=0, keepdims=True)

    which = lax.broadcasted_iota(jnp.int32, (ANG, parts), 0)
    owner = jnp.where((which == (target >> 7)) & live, 1.0, 0.0)
    row = jnp.where(which == (target & 127), 1.0, 0.0).astype(BF16)
    rest = loglik
    table = jnp.zeros((ANG, ANG), F32)
    for _ in range(3):
        piece = rest.astype(BF16).astype(F32)
        table += lax.dot_general((owner * piece).astype(BF16), row, (((1,), (1,)), ((), ())), preferred_element_type=F32)
        rest = rest - piece
    ll_out[...] = table

    def collect(g, _):
        cols = pl.ds(pl.multiple_of(g * 2 * ANG, 2 * ANG), 2 * ANG)
        h = jnp.dot(weights[...], shifted[:, cols], preferred_element_type=F32)
        for k in range(2):
            sum0 = jnp.zeros((CPAD, ANG), F32)
            sum1 = jnp.zeros((CPAD, ANG), F32)
            for i, (first, w0, w1) in enumerate(TAPS):
                q = h[i * CPAD : (i + 1) * CPAD, k * ANG : (k + 1) * ANG]
                if first:
                    q = pltpu.roll(q, ANG - first, 1)
                sum0 += w0 * q
                if w1:
                    sum1 += w1 * q
            g_out[2 * g + k, :, :] = sum0 + pltpu.roll(sum1, ANG - 1, 1)
        return 0

    lax.fori_loop(0, RAD // 2, collect, 0)


def local_terms(micrographs, positions, counts, dest_rows, templates):
    mics, slots = dest_rows.shape
    parts = mics * slots
    cells = RAD * ANG
    ys, xs = sample_points()
    vmem = pl.BlockSpec(memory_space=pltpu.VMEM)
    smem = pl.BlockSpec(memory_space=pltpu.SMEM)
    return pl.pallas_call(
        local_kernel,
        out_shape=(
            jax.ShapeDtypeStruct((RAD, CPAD, ANG), F32),
            jax.ShapeDtypeStruct((1, ANG), F32),
            jax.ShapeDtypeStruct((ANG, ANG), F32),
        ),
        in_specs=[smem, smem, pl.BlockSpec(memory_space=pl.ANY), vmem, vmem, vmem, vmem],
        out_specs=(vmem, vmem, vmem),
        scratch_shapes=[
            pltpu.VMEM((2, 1024, 1024), BF16),
            pltpu.VMEM((8, 1024, ANG), F32),
            pltpu.VMEM((BOX // 2 * parts, ANG), F32),
            pltpu.VMEM((parts, BOX * BOX), BF16),
            pltpu.VMEM((2, BOX * BOX, 2 * ANG), BF16),
            pltpu.VMEM((CPAD * RAD, ANG), F32),
            pltpu.VMEM((NROWS, cells), BF16),
            pltpu.VMEM((NROWS, ANG), F32),
            pltpu.VMEM((QROT * parts, cells), BF16),
            pltpu.VMEM((NROWS, QROT * parts), F32),
            pltpu.VMEM((NROWS, QROT * parts), BF16),
            pltpu.VMEM((NROWS, ANG), F32),
            pltpu.SemaphoreType.DMA((2,)),
        ],
        compiler_params=pltpu.CompilerParams(vmem_limit_bytes=60 * 1024 * 1024),
        name="local_terms",
    )(positions, counts, micrographs, dest_rows.reshape(1, parts), jnp.asarray(ys), jnp.asarray(xs), templates)


DEVICES = 128


def on_device(micrographs, positions, counts, dest_rows, templates):
    sums, tot, table = local_terms(micrographs, positions, counts, dest_rows, templates)
    packed = jnp.concatenate([sums.reshape(-1, ANG), tot, table], axis=0)
    packed = lax.psum(packed, "dev")
    sums = packed[: RAD * CPAD].reshape(RAD, CPAD, ANG)[:, :CLASSES]
    tot = packed[RAD * CPAD, :CLASSES]
    means = sums.transpose(1, 0, 2) / jnp.maximum(tot, 1.0)[:, None, None]
    table = packed[RAD * CPAD + 1 :]
    mine = lax.dynamic_slice(table, (lax.axis_index("dev"), 0), (1, ANG))[0]
    return means, mine


def solution(mesh):
    P = jax.sharding.PartitionSpec
    return jax.shard_map(
        on_device,
        mesh=mesh,
        in_specs=(P("dev", None, None), P(None, "dev", None), P("dev"), P("dev", None), P()),
        out_specs=(P(), P("dev")),
        check_vma=False,
    )
```

profile of v0, /device:TPU:1, one launch (start us, length us, event | category | flops | bytes accessed | tf_op | source)
XLA Modules:
  0.0 235.6 jit_solution(5683680102559089643)
XLA Ops:
  7.2 0.0 all-reduce.2.cloned.1.call-start
  7.2 1.3 reshape.20.dest
  8.5 53.6 %local_terms.1 = (f32[32,104,128]{2,1,0:T(8,128)}, f32[1,128]{1,0:T(1,128)}, f32[128,128]{1,0:T(8,128)}) custom-call(s32[2,4,64]{2,1,0:T(4,128)} %pos.1, s32[4]{0:T(128)} %counts.1, bf16[4,1024,1024]{2,1,0:T(8,128)(2,1)} %mic.1, s32[1,256]{1,0:T(1,128)} %reshape.20.dest, f32[1,4096]{1,0:T(1,128)} %constant.14.clone.ys, f32[1,4096]{1,0:T(1,128)} %constant.15.clone.xs, ...), custom_call_target="tpu_custom_call" | custom-call | tf_op jit(solution)/shard_map/local_terms/pallas_call | solution.py:218
  62.2 7.7 %concatenate.3 = f32[3457,128]{1,0:T(8,128)} concatenate(f32[3328,128]{1,0:T(8,128)} %bitcast.9, f32[1,128]{1,0:T(1,128)} %get-tuple-element.6, f32[128,128]{1,0:T(8,128)} %get-tuple-element.7), dimensions={0} | concatenate | bytes 3539968 | tf_op jit(solution)/shard_map/concatenate | solution.py:252
  69.9 0.0 all-reduce.2.cloned.1.call-update
  69.9 154.0 %all-reduce.2.cloned.1.call-done = f32[3457,128]{1,0:T(8,128)} async-done(((f32[3457,128]{1,0:T(8,128)}), f32[3457,128]{1,0:T(8,128)}) %all-reduce.2.cloned.1.call-update) | async-done | bytes 1770000 | tf_op jit(solution)/shard_map/psum | solution.py:253
  223.9 0.7 fusion.1
  224.6 0.0 slice-start
  224.6 1.5 slice-done
  226.0 0.2 fusion
  226.2 0.0 copy-start
  226.2 1.5 copy.9
  227.7 0.5 copy-done
  228.2 0.5 dynamic-slice_bitcast_fusion
  (1 shorter events, 0.0 us)
Async XLA Ops:
  7.2 216.7 %all-reduce.2.cloned.1.call-start = ((), (), s32[]{:S(2)}) async-start(), calls=%async_computation | async-start | bytes 3547136 | tf_op jit(solution)/shard_map/psum | solution.py:253
  224.6 1.5 slice-start
  226.2 2.0 copy-start
Sparse Core Ops, SparseCore 0:
  70.0 153.8 all-reduce.1
where the time goes:
time: 236 us
  waiting for transfers between devices  154 us (65%)
  Pallas kernels  53.6 us (23%)
  between operations  14.1 us (6%)
  local copies, waits for them, and re-layouts  13 us (6%)
    psum x1, waiting for transfers between devices, on_device(): packed = lax.psum(packed, 'dev')  154 us
    pallas_call x1, Pallas kernels, local_terms(): pl.pallas_call(local_kernel, out_shape=(jax.ShapeDtypeStruct((RAD, CPAD,...  53.6 us
    concatenate x1, local copies, waits for them, and re-layouts, on_device(): packed = jnp.concatenate([sums.reshape(-1, ANG), tot, table], axis=0)  7.71 us
  transfers between devices with their start and end apart: 1, of which 1 were waited for; matrix products, arithmetic and copies ran while one was open for 0% of the time, Pallas kernels for 0%

commit v1 on v0

--- a/solution.py
+++ b/solution.py
@@ -15,6 +15,9 @@
 QROT = 4
 BASE = 9
 NROWS = 4 * 2 * CPAD + 112
+DEVICES = 128
+CHIPS = DEVICES // 2
+PIECE = 32
 F32 = jnp.float32
 BF16 = jnp.bfloat16
 
@@ -44,8 +47,7 @@
 TAPS = rotation_taps()
 
 
-def local_kernel(pos, counts, mic, dest, ys, xs, tmpl, g_out, tot_out, ll_out,
-                 raw, planes, flat, boxes, wtile, tflat, rot, esum, shifted, scores, weights, tsum, sems):
+def local_kernel(pos, counts, mic, dest, ys, xs, tmpl, out, extra, raw, planes, flat, boxes, wtile, tflat, rot, esum, shifted, scores, weights, tsum, sems):
     mics = mic.shape[0]
     slots = pos.shape[2]
     parts = mics * slots
@@ -176,18 +178,26 @@
     tot = jnp.sum(tsum[...], axis=1, keepdims=True)
     tot = sum(tot[i * CPAD : (i + 1) * CPAD] for i in range(BASE))
     spot = lax.broadcasted_iota(jnp.int32, (CPAD, ANG), 0) == lax.broadcasted_iota(jnp.int32, (CPAD, ANG), 1)
-    tot_out[...] = jnp.sum(jnp.where(spot, tot, 0.0), axis=0, keepdims=True)
+    tot = jnp.sum(jnp.where(spot, tot, 0.0), axis=0, keepdims=True)
+    high = tot.astype(BF16).astype(F32)
+    first = lax.rem(lax.axis_index("dev"), 2) == 0
+    extra[...] = jnp.zeros_like(extra)
+    for value, here, there in ((high, 1, 6), (tot - high, 2, 7)):
+        value = jnp.broadcast_to(value, (DEVICES, ANG))
+        extra[pl.ds(here, DEVICES, stride=8), :] = jnp.where(first, value, 0.0)
+        extra[pl.ds(there, DEVICES, stride=8), :] = jnp.where(first, 0.0, value)
 
     which = lax.broadcasted_iota(jnp.int32, (ANG, parts), 0)
     owner = jnp.where((which == (target >> 7)) & live, 1.0, 0.0)
     row = jnp.where(which == (target & 127), 1.0, 0.0).astype(BF16)
     rest = loglik
-    table = jnp.zeros((ANG, ANG), F32)
-    for _ in range(3):
+    for k in range(3):
         piece = rest.astype(BF16).astype(F32)
-        table += lax.dot_general((owner * piece).astype(BF16), row, (((1,), (1,)), ((), ())), preferred_element_type=F32)
+        table = lax.dot_general((owner * piece).astype(BF16), row, (((1,), (1,)), ((), ())), preferred_element_type=F32)
+        extra[pl.ds(3 + k, DEVICES, stride=8), :] = table
         rest = rest - piece
-    ll_out[...] = table
+
+    top = lax.broadcasted_iota(jnp.int32, (8, ANG), 0)
 
     def collect(g, _):
         cols = pl.ds(pl.multiple_of(g * 2 * ANG, 2 * ANG), 2 * ANG)
@@ -202,7 +212,14 @@
                 sum0 += w0 * q
                 if w1:
                     sum1 += w1 * q
-            g_out[2 * g + k, :, :] = sum0 + pltpu.roll(sum1, ANG - 1, 1)
+            total = sum0 + pltpu.roll(sum1, ANG - 1, 1)
+            r = 2 * g + k
+            for q in range(4):
+                tail = total[96:] if q == 0 else pltpu.roll(total[96:], 8 - q, 0)
+                spare = extra[pl.ds(pl.multiple_of((4 * r + q) * 8, 8), 8), :]
+                tail = jnp.where(top == 0, tail, spare)
+                piece = jnp.concatenate([total[24 * q : 24 * q + 24], tail], axis=0)
+                out[q % 2, 2 * r + q // 2, :, :] = piece.astype(BF16)
         return 0
 
     lax.fori_loop(0, RAD // 2, collect, 0)
@@ -217,14 +234,11 @@
     smem = pl.BlockSpec(memory_space=pltpu.SMEM)
     return pl.pallas_call(
         local_kernel,
-        out_shape=(
-            jax.ShapeDtypeStruct((RAD, CPAD, ANG), F32),
-            jax.ShapeDtypeStruct((1, ANG), F32),
-            jax.ShapeDtypeStruct((ANG, ANG), F32),
-        ),
+        out_shape=jax.ShapeDtypeStruct((2, DEVICES // 2, PIECE, ANG), BF16),
         in_specs=[smem, smem, pl.BlockSpec(memory_space=pl.ANY), vmem, vmem, vmem, vmem],
-        out_specs=(vmem, vmem, vmem),
+        out_specs=vmem,
         scratch_shapes=[
+            pltpu.VMEM((DEVICES * 8, ANG), F32),
             pltpu.VMEM((2, 1024, 1024), BF16),
             pltpu.VMEM((8, 1024, ANG), F32),
             pltpu.VMEM((BOX // 2 * parts, ANG), F32),
@@ -244,19 +258,161 @@
     )(positions, counts, micrographs, dest_rows.reshape(1, parts), jnp.asarray(ys), jnp.asarray(xs), templates)
 
 
-DEVICES = 128
+def remote(src, dst, send_sem, recv_sem, device):
+    return pltpu.make_async_remote_copy(
+        src_ref=src,
+        dst_ref=dst,
+        send_sem=send_sem,
+        recv_sem=recv_sem,
+        device_id=(device,),
+        device_id_type=pl.DeviceIdType.MESH,
+    )
+
+
+def combine_kernel(packed, means, loglik, own, half, send, landed, gathered, crossed,
+                   own_sem, half_send, half_recv, put_send, put_recv, get_send, get_recv, cross_send, cross_recv):
+    me = lax.axis_index("dev")
+    core = lax.rem(me, 2)
+    chip = me // 2
+    partner = me + 1 - 2 * core
+    chunk = CHIPS // 4
+
+    local = pltpu.make_async_copy(packed.at[core], own, own_sem)
+    local.start()
+
+    barrier = pltpu.get_barrier_semaphore()
+    pl.semaphore_signal(barrier, inc=1, device_id=(partner,), device_id_type=pl.DeviceIdType.MESH)
+
+    def greet(k, _):
+        pl.semaphore_signal(
+            barrier, inc=1, device_id=(2 * (chip ^ k) + core,), device_id_type=pl.DeviceIdType.MESH
+        )
+        return 0
+
+    lax.fori_loop(1, CHIPS, greet, 0)
+    pl.semaphore_wait(barrier, CHIPS)
+
+    def half_copy(b):
+        at = pl.ds((chip // chunk ^ b) * chunk, chunk)
+        return remote(packed.at[1 - core, at], half.at[at], half_send.at[b], half_recv.at[b], partner)
+
+    for b in range(4):
+        half_copy(b).start()
+    local.wait()
+
+    def put(c, device_chip):
+        return remote(
+            send.at[c], landed.at[device_chip], put_send.at[c], put_recv.at[device_chip], 2 * c + core
+        )
+
+    for b in range(4):
+        half_copy(b).wait_recv()
+
+        def give(k, _, b=b):
+            c = (chip // chunk ^ b) * chunk + (lax.rem(chip, chunk) ^ k)
+            send[c] = (own[c].astype(F32) + half[c].astype(F32)).astype(BF16)
+
+            @pl.when(c != chip)
+            def _():
+                put(c, chip).start()
+
+            return 0
+
+        lax.fori_loop(0, chunk, give, 0)
+
+    def take(k, acc):
+        c = chip ^ k
+        remote(send.at[c], landed.at[c], put_send.at[c], put_recv.at[c], 2 * c + core).wait_recv()
+        return acc + landed[c].astype(F32)
+
+    acc = lax.fori_loop(1, CHIPS, take, send[chip].astype(F32))
+
+    quarter = 2 * lax.rem(chip, 2) + core
+    row = lax.broadcasted_iota(jnp.int32, (PIECE, ANG), 0)
+    lane = lax.broadcasted_iota(jnp.int32, (PIECE, ANG), 1)
+    which = jnp.where(row < 24, 24 * quarter + row, 96 + quarter)
+    total = acc[25:26] + acc[26:27] + acc[30:31] + acc[31:32]
+    total = jnp.sum(jnp.where(lane == which, total, 0.0), axis=1, keepdims=True)
+    gathered[chip] = (acc / jnp.maximum(total, 1.0)).astype(BF16)
+    loglik[...] = acc[27:28] + acc[28:29] + acc[29:30]
+
+    def share(c, to):
+        return remote(gathered.at[c], gathered.at[c], get_send.at[to], get_recv.at[c], 2 * to + core)
+
+    def pass_on(c):
+        return remote(gathered.at[c], crossed.at[c], cross_send.at[c], cross_recv.at[c], partner)
+
+    def spread(k, _):
+        share(chip, chip ^ k).start()
+        return 0
+
+    lax.fori_loop(1, CHIPS, spread, 0)
+    pass_on(chip).start()
+
+    def write(piece, c, k):
+        r = c // 2
+        q = 2 * lax.rem(c, 2) + k
+        wide = piece.astype(F32)
+        means[pl.ds(24 * RAD * q + r, 24, stride=RAD), :] = wide[:24]
+        means[pl.ds((96 + q) * RAD + r, 1), :] = wide[24:25]
+
+    write(gathered[chip], chip, core)
+
+    def collect(k, _):
+        c = chip ^ k
+        share(c, c).wait_recv()
+        pass_on(c).start()
+        write(gathered[c], c, core)
+        return 0
+
+    lax.fori_loop(1, CHIPS, collect, 0)
+
+    def cross(k, _):
+        c = chip ^ k
+        pass_on(c).wait_recv()
+        write(crossed[c], c, 1 - core)
+        return 0
+
+    lax.fori_loop(0, CHIPS, cross, 0)
+
+    for b in range(4):
+        half_copy(b).wait_send()
+
+    def drain(k, _):
+        c = chip ^ k
+        put(c, chip).wait_send()
+        share(chip, c).wait_send()
+        pass_on(c).wait_send()
+        return 0
+
+    lax.fori_loop(1, CHIPS, drain, 0)
+    pass_on(chip).wait_send()
+
+
+def combine(packed):
+    block = pltpu.VMEM((CHIPS, PIECE, ANG), BF16)
+    many = pltpu.SemaphoreType.DMA((CHIPS,))
+    vmem = pl.BlockSpec(memory_space=pltpu.VMEM)
+    return pl.pallas_call(
+        combine_kernel,
+        out_shape=(
+            jax.ShapeDtypeStruct((CLASSES * RAD, ANG), F32),
+            jax.ShapeDtypeStruct((1, ANG), F32),
+        ),
+        in_specs=[pl.BlockSpec(memory_space=pl.ANY)],
+        out_specs=(vmem, vmem),
+        scratch_shapes=[block] * 6
+        + [pltpu.SemaphoreType.DMA, pltpu.SemaphoreType.DMA((4,)), pltpu.SemaphoreType.DMA((4,))]
+        + [many] * 6,
+        compiler_params=pltpu.CompilerParams(collective_id=0, has_side_effects=True),
+        name="combine",
+    )(packed)
 
 
 def on_device(micrographs, positions, counts, dest_rows, templates):
-    sums, tot, table = local_terms(micrographs, positions, counts, dest_rows, templates)
-    packed = jnp.concatenate([sums.reshape(-1, ANG), tot, table], axis=0)
-    packed = lax.psum(packed, "dev")
-    sums = packed[: RAD * CPAD].reshape(RAD, CPAD, ANG)[:, :CLASSES]
-    tot = packed[RAD * CPAD, :CLASSES]
-    means = sums.transpose(1, 0, 2) / jnp.maximum(tot, 1.0)[:, None, None]
-    table = packed[RAD * CPAD + 1 :]
-    mine = lax.dynamic_slice(table, (lax.axis_index("dev"), 0), (1, ANG))[0]
-    return means, mine
+    packed = local_terms(micrographs, positions, counts, dest_rows, templates)
+    means, loglik = combine(packed)
+    return means.reshape(CLASSES, RAD, ANG), loglik.reshape(ANG)
 
 
 def solution(mesh):

time: 236 us -> 100 us (0.42)
  waiting for transfers between devices: 154 us -> 0 us
  Pallas kernels: 53.6 us -> 94.7 us
  between operations: 14.1 us -> 0.65 us
  local copies, waits for them, and re-layouts: 13 us -> 4.56 us
    psum x1 -> x0, waiting for transfers between devices: 154 us -> none  [on_device(): packed = lax.psum(packed, 'dev')]
    pallas_call x1 -> x2, Pallas kernels: 53.6 us -> 94.7 us  [the longest x1 53.5 us: local_terms(): pl.pallas_call(local_kernel, out_shape=jax.ShapeDtypeStruct((2, DEVICES /...]
    concatenate x1 -> x0, local copies, waits for them, and re-layouts: 7.71 us -> none  [on_device(): packed = jnp.concatenate([sums.reshape(-1, ANG), tot, table], axis=0)]
  transfers between devices with their start and end apart: 1 -> 0, of which waited for: 1 -> 0; matrix products, arithmetic and copies ran while one was open for 0% -> 0% of each run, Pallas kernels for 0% -> 0%
where the time goes in v1:
time: 100 us
  Pallas kernels  94.7 us (95%)
  local copies, waits for them, and re-layouts  4.56 us (5%)
    pallas_call x1, Pallas kernels, local_terms(): pl.pallas_call(local_kernel, out_shape=jax.ShapeDtypeStruct((2, DEVICES /...  53.5 us
    pallas_call x1, Pallas kernels, combine(): pl.pallas_call(combine_kernel, out_shape=(jax.ShapeDtypeStruct((CLASSES *...  41.2 us
    unnamed x4, local copies, waits for them, and re-layouts  3.24 us

profile of v1, /device:TPU:1, one launch (start us, length us, event | category | flops | bytes accessed | tf_op | source)
XLA Modules:
  0.0 100.0 jit_solution(1777895708941669605)
XLA Ops:
  0.6 1.3 %reshape.13.dest = s32[1,256]{1,0:T(1,128)} reshape(s32[4,64]{1,0:T(4,128)} %param.10) | data formatting | bytes 2048 | tf_op jit(solution)/shard_map/reshape | solution.py:258
  2.0 53.5 %local_terms.1.packed = bf16[2,64,32,128]{3,2,1,0:T(8,128)(2,1)} custom-call(s32[2,4,64]{2,1,0:T(4,128)} %pos.1, s32[4]{0:T(128)} %counts.1, bf16[4,1024,1024]{2,1,0:T(8,128)(2,1)} %mic.1, s32[1,256]{1,0:T(1,128)} %reshape.13.dest, f32[1,4096]{1,0:T(1,128)} %constant.4.clone.ys, f32[1,4096]{1,0:T(1,128)} %constant.5.clone.xs, bf16[100,32,128]{2,1,0:T(8,128)(2,1)} %tmpl.1), custom_call_target="tpu_custom_call" | custom-call | tf_op jit(solution)/shard_map/local_terms/pallas_call | solution.py:235
  55.5 41.2 %combine.1 = (f32[3200,128]{1,0:T(8,128)}, f32[1,128]{1,0:T(1,128)}) custom-call(bf16[2,64,32,128]{3,2,1,0:T(8,128)(2,1)} %local_terms.1.packed), custom_call_target="tpu_custom_call" | custom-call | tf_op jit(solution)/shard_map/combine/pallas_call | solution.py:396
  96.7 0.0 copy-start
  96.7 2.7 %copy.11 = f32[100,32,128]{2,1,0:T(8,128)} copy(f32[100,32,128]{2,1,0:T(8,128)} %bitcast.2) | data formatting | bytes 3276800
  99.4 0.0 copy-done
  99.4 0.5 copy.12
Async XLA Ops:
  96.7 2.7 %copy-start = (f32[1,128]{1,0:T(1,128)S(1)}, f32[1,128]{1,0:T(1,128)}, u32[]{:S(2)}) copy-start(f32[1,128]{1,0:T(1,128)} %get-tuple-element.5) | copy-start | bytes 1540

commit v2 on v1

--- a/solution.py
+++ b/solution.py
@@ -28,7 +28,13 @@
     theta = np.float32(2.0 * np.pi) * np.arange(ANG, dtype=np.float32) / np.float32(ANG)
     ys = (center + radius[:, None] * np.sin(theta)[None, :]).reshape(1, -1)
     xs = (center + radius[:, None] * np.cos(theta)[None, :]).reshape(1, -1)
-    return ys.astype(np.float32), xs.astype(np.float32)
+    def ordered(v):
+        v = v.astype(np.float32).reshape(RAD // 4, 2, 2, 2, ANG // 2)
+        v = v.transpose(0, 3, 1, 2, 4)
+        v = np.stack([v[:, 0], v[:, 1, :, ::-1]], axis=1)
+        return v.reshape(1, -1)
+
+    return ordered(ys), ordered(xs)
 
 
 def rotation_taps():
@@ -47,7 +53,14 @@
 TAPS = rotation_taps()
 
 
-def local_kernel(pos, counts, mic, dest, ys, xs, tmpl, out, extra, raw, planes, flat, boxes, wtile, tflat, rot, esum, shifted, scores, weights, tsum, sems):
+def turned_rows(x, i):
+    if i == 8:
+        return x[8 * CPAD : 9 * CPAD]
+    pair = x[(i // 2) * 2 * CPAD : (i // 2 + 1) * 2 * CPAD].reshape(CPAD // 8, 16, x.shape[1])
+    return pair[:, 8 * (i % 2) : 8 * (i % 2) + 8].reshape(CPAD, x.shape[1])
+
+
+def local_kernel(pos, counts, mic, dest, ys, xs, tmpl, out, extra, raw, planes, flat, boxes, wtile, tflat, rot, esum, shifted, scores, weights, tsum, sums_a, sums_b, sems):
     mics = mic.shape[0]
     slots = pos.shape[2]
     parts = mics * slots
@@ -60,28 +73,41 @@
 
     lane1 = lax.broadcasted_iota(jnp.int32, (1, ANG), 1)
 
-    tflat[pl.ds(CLASSES * RAD, (CPAD - CLASSES) * RAD), :] = jnp.zeros(((CPAD - CLASSES) * RAD, ANG), F32)
+    tflat[pl.ds(CLASSES * RAD, 12 * RAD), :] = jnp.zeros((12 * RAD, ANG), F32)
     tflat[pl.ds(0, CLASSES * RAD), :] = tmpl[...].reshape(CLASSES * RAD, ANG).astype(F32)
-    esum[...] = jnp.zeros_like(esum)
-    rot[pl.ds(8 * CPAD, 112), :] = jnp.zeros((112, RAD * ANG), BF16)
-
-    def rotate_radius(r, _):
-        x = tflat[pl.ds(r, CPAD, stride=RAD), :]
-        x1 = pltpu.roll(x, 1, 1)
-        col = pl.ds(pl.multiple_of(r * ANG, ANG), ANG)
-        turned = []
-        for first, w0, w1 in TAPS:
-            y = x if w1 == 0.0 else w0 * x + w1 * x1
-            turned.append(pltpu.roll(y, first, 1) if first else y)
-        turned.append(jnp.zeros((8, ANG), F32))
-        for i in range(0, BASE, 2):
-            pair = jnp.concatenate(turned[i : i + 2], axis=0).astype(BF16)
-            rot[pl.ds(i * CPAD, pair.shape[0]), col] = pair
-            wide = pair.astype(F32)
-            esum[pl.ds(i * CPAD, pair.shape[0]), :] += wide * wide
-        return 0
-
-    lax.fori_loop(0, RAD, rotate_radius, 0)
+
+    def rotate_tile(n, _):
+        t = 6 - n
+        starts = [pl.multiple_of(k * 2 * CPAD + (2 * t + h) * 16, 16) for k in range(4) for h in range(2)]
+        starts.append(pl.multiple_of(8 * CPAD + t * 16, 16))
+
+        def rotate_radius(r, sums):
+            x = tflat[pl.ds(t * 16 * RAD + r, 16, stride=RAD), :]
+            x1 = pltpu.roll(x, 1, 1)
+            col = pl.ds(pl.multiple_of(r * ANG, ANG), ANG)
+            turned = []
+            for first, w0, w1 in TAPS:
+                y = x if w1 == 0.0 else w0 * x + w1 * x1
+                turned.append(pltpu.roll(y, first, 1) if first else y)
+            tiles = [
+                jnp.concatenate([turned[2 * k][8 * h : 8 * h + 8], turned[2 * k + 1][8 * h : 8 * h + 8]], axis=0)
+                for k in range(4)
+                for h in range(2)
+            ] + [turned[8]]
+            new = []
+            for start, tile, total in zip(starts, tiles, sums):
+                tile = tile.astype(BF16)
+                rot[pl.ds(start, 16), col] = tile
+                wide = tile.astype(F32)
+                new.append(total + wide * wide)
+            return tuple(new)
+
+        sums = lax.fori_loop(0, RAD, rotate_radius, (jnp.zeros((16, ANG), F32),) * 9, unroll=2)
+        for start, total in zip(starts, sums):
+            esum[pl.ds(start, 16), :] = total
+        return 0
+
+    lax.fori_loop(0, 7, rotate_tile, 0)
 
     lanes = lax.broadcasted_iota(jnp.int32, (BOX // 2, ANG), 1)
     for i in range(mics):
@@ -94,47 +120,60 @@
         def cut(j, _, i=i):
             y = pos[0, i, j]
             x = pos[1, i, j]
-            t = x // ANG
-            s = x - t * ANG
+            t = x >> 7
+            s = x & 127
             t1 = jnp.minimum(t + 1, 7)
             even = pl.ds(y, BOX // 2, stride=2)
             odd = pl.ds(y + 1, BOX // 2, stride=2)
             keep = lanes >= s
             e = jnp.where(keep, planes[t, even, :], planes[t1, even, :])
             o = jnp.where(keep, planes[t, odd, :], planes[t1, odd, :])
-            e = pltpu.roll(e, lax.rem(ANG - s, ANG), 1)
-            o = pltpu.roll(o, lax.rem(ANG + BOX - s, ANG), 1)
+            e = pltpu.roll(e, (ANG - s) & 127, 1)
+            o = pltpu.roll(o, (ANG + BOX - s) & 127, 1)
             flat[pl.ds(i * slots + j, BOX // 2, stride=parts), :] = jnp.where(lanes < BOX, e, o)
             return 0
 
-        lax.fori_loop(0, slots, cut, 0, unroll=4)
+        lax.fori_loop(0, slots, cut, 0, unroll=8)
 
     for s in range(BOX // 2):
         boxes[:, s * ANG : (s + 1) * ANG] = flat[pl.ds(s * parts, parts), :].astype(BF16)
 
     pix = lax.broadcasted_iota(jnp.int32, (BOX, 2 * ANG), 0).astype(F32)
-    for g in range(RAD // 2):
-        radius = (2 * g + 1.5) * (BOX / 2.0 - 1.0) / RAD
-        low = int(np.floor(31.5 - radius)) - 1
-        low = max(0, low // 4 * 4)
-        high = BOX - low
-        cols = slice(g * 2 * ANG, (g + 1) * 2 * ANG)
-        rw = jnp.maximum(0.0, 1.0 - jnp.abs(pix - ys[:, cols]))
-        cw = jnp.maximum(0.0, 1.0 - jnp.abs(pix - xs[:, cols]))
-        w = wtile.at[g % 2]
-        for u in range(low, high):
-            w[u * BOX : (u + 1) * BOX, :] = (rw[u : u + 1, :] * cw).astype(BF16)
-        p = jnp.dot(boxes[:, low * BOX : high * BOX], w[low * BOX : high * BOX, :], preferred_element_type=F32)
-        for h in range(2):
-            half = p[:, h * ANG : (h + 1) * ANG]
-            c0 = (2 * g + h) * ANG
-            for j in range(QROT):
-                part = half if j == 0 else pltpu.roll(half, ANG - 32 * j, 1)
-                shifted[j * parts : (j + 1) * parts, c0 : c0 + ANG] = part.astype(BF16)
+    left = lax.broadcasted_iota(jnp.int32, (parts, ANG), 1) < BOX
+    for g in range(RAD // 4):
+        radius = (4 * g + 3.5) * (BOX / 2.0 - 1.0) / RAD
+        reach = (int(np.floor(31.501 + radius)) + 3) // 2 * 2
+        halves = []
+        for side in range(2):
+            low, high = (30, reach) if side == 0 else (BOX - reach, 34)
+            cols = slice((2 * g + side) * 2 * ANG, (2 * g + side + 1) * 2 * ANG)
+            rw = jnp.maximum(0.0, 1.0 - jnp.abs(pix - ys[:, cols]))
+            cw = jnp.maximum(0.0, 1.0 - jnp.abs(pix - xs[:, cols]))
+            w = wtile.at[side]
+            for u in range(low, high):
+                w[(u - low) * BOX : (u - low + 1) * BOX, :] = (rw[u : u + 1, :] * cw).astype(BF16)
+            halves.append(
+                jnp.dot(
+                    boxes[:, low * BOX : high * BOX],
+                    w[: (high - low) * BOX, :],
+                    preferred_element_type=F32,
+                )
+            )
+        for m in range(2):
+            upper = halves[0][:, m * ANG : (m + 1) * ANG]
+            lower = halves[1][:, m * ANG : (m + 1) * ANG]
+            for h in range(2):
+                whole = jnp.where(left, upper, lower) if h == 0 else jnp.where(left, lower, upper)
+                c0 = (4 * g + 2 * m + h) * ANG
+                for j in range(QROT):
+                    turn = (BOX * h - 32 * j) % ANG
+                    part = pltpu.roll(whole, turn, 1) if turn else whole
+                    shifted[j * parts : (j + 1) * parts, c0 : c0 + ANG] = part.astype(BF16)
 
     rows = lax.broadcasted_iota(jnp.int32, (NROWS, 1), 0)
     energy = 0.5 * jnp.sum(esum[...], axis=1, keepdims=True)
-    pad = (lax.rem(rows, CPAD) >= CLASSES) | (rows >= BASE * CPAD)
+    paired = lax.rem(rows >> 4, 13) * 8 + (rows & 7)
+    pad = jnp.where(rows < 8 * CPAD, paired, rows - 8 * CPAD) >= CLASSES
     energy = jnp.where(pad, 1e30, energy)
 
     def score(j, peak):
@@ -159,7 +198,7 @@
     loglik = peak + jnp.log(norm)
 
     lane = lax.broadcasted_iota(jnp.int32, (1, parts), 1)
-    target = dest[...]
+    target = jnp.concatenate([dest[i : i + 1, :] for i in range(mics)], axis=1)
     live = target >= 0
     for i in range(mics):
         live = live & ((lane < i * slots + counts[i]) | (lane >= (i + 1) * slots))
@@ -175,8 +214,7 @@
         return 0
 
     lax.fori_loop(0, NROWS // 16, weigh, 0)
-    tot = jnp.sum(tsum[...], axis=1, keepdims=True)
-    tot = sum(tot[i * CPAD : (i + 1) * CPAD] for i in range(BASE))
+    tot = jnp.sum(sum(turned_rows(tsum[...], i) for i in range(BASE)), axis=1, keepdims=True)
     spot = lax.broadcasted_iota(jnp.int32, (CPAD, ANG), 0) == lax.broadcasted_iota(jnp.int32, (CPAD, ANG), 1)
     tot = jnp.sum(jnp.where(spot, tot, 0.0), axis=0, keepdims=True)
     high = tot.astype(BF16).astype(F32)
@@ -199,14 +237,17 @@
 
     top = lax.broadcasted_iota(jnp.int32, (8, ANG), 0)
 
-    def collect(g, _):
+    def product(g, into):
         cols = pl.ds(pl.multiple_of(g * 2 * ANG, 2 * ANG), 2 * ANG)
-        h = jnp.dot(weights[...], shifted[:, cols], preferred_element_type=F32)
+        into[...] = jnp.dot(weights[...], shifted[:, cols], preferred_element_type=F32)
+
+    def fold(g, source):
         for k in range(2):
             sum0 = jnp.zeros((CPAD, ANG), F32)
             sum1 = jnp.zeros((CPAD, ANG), F32)
+            half = source[:, k * ANG : (k + 1) * ANG]
             for i, (first, w0, w1) in enumerate(TAPS):
-                q = h[i * CPAD : (i + 1) * CPAD, k * ANG : (k + 1) * ANG]
+                q = turned_rows(half, i)
                 if first:
                     q = pltpu.roll(q, ANG - first, 1)
                 sum0 += w0 * q
@@ -220,9 +261,20 @@
                 tail = jnp.where(top == 0, tail, spare)
                 piece = jnp.concatenate([total[24 * q : 24 * q + 24], tail], axis=0)
                 out[q % 2, 2 * r + q // 2, :, :] = piece.astype(BF16)
-        return 0
-
-    lax.fori_loop(0, RAD // 2, collect, 0)
+
+    product(0, sums_a)
+
+    def collect(n, _):
+        product(2 * n + 1, sums_b)
+        fold(2 * n, sums_a)
+        product(2 * n + 2, sums_a)
+        fold(2 * n + 1, sums_b)
+        return 0
+
+    lax.fori_loop(0, RAD // 4 - 1, collect, 0)
+    product(RAD // 2 - 1, sums_b)
+    fold(RAD // 2 - 2, sums_a)
+    fold(RAD // 2 - 1, sums_b)
 
 
 def local_terms(micrographs, positions, counts, dest_rows, templates):
@@ -243,19 +295,21 @@
             pltpu.VMEM((8, 1024, ANG), F32),
             pltpu.VMEM((BOX // 2 * parts, ANG), F32),
             pltpu.VMEM((parts, BOX * BOX), BF16),
-            pltpu.VMEM((2, BOX * BOX, 2 * ANG), BF16),
-            pltpu.VMEM((CPAD * RAD, ANG), F32),
+            pltpu.VMEM((2, 34 * BOX, 2 * ANG), BF16),
+            pltpu.VMEM((112 * RAD, ANG), F32),
             pltpu.VMEM((NROWS, cells), BF16),
             pltpu.VMEM((NROWS, ANG), F32),
             pltpu.VMEM((QROT * parts, cells), BF16),
             pltpu.VMEM((NROWS, QROT * parts), F32),
             pltpu.VMEM((NROWS, QROT * parts), BF16),
             pltpu.VMEM((NROWS, ANG), F32),
+            pltpu.VMEM((NROWS, 2 * ANG), F32),
+            pltpu.VMEM((NROWS, 2 * ANG), F32),
             pltpu.SemaphoreType.DMA((2,)),
         ],
         compiler_params=pltpu.CompilerParams(vmem_limit_bytes=60 * 1024 * 1024),
         name="local_terms",
-    )(positions, counts, micrographs, dest_rows.reshape(1, parts), jnp.asarray(ys), jnp.asarray(xs), templates)
+    )(positions, counts, micrographs, dest_rows, jnp.asarray(ys), jnp.asarray(xs), templates)
 
 
 def remote(src, dst, send_sem, recv_sem, device):

time: 100 us -> 102 us (1.020)
  Pallas kernels: 94.7 us -> 97.7 us
  local copies, waits for them, and re-layouts: 4.56 us -> 3.24 us
    pallas_call x1, Pallas kernels: 53.5 us -> 56.5 us  [local_terms(): pl.pallas_call(local_kernel, out_shape=jax.ShapeDtypeStruct((2, DEVICES /...]
    reshape x1 -> x0, local copies, waits for them, and re-layouts: 1.32 us -> none  [local_terms(): dest_rows.reshape(1, parts)]
where the time goes in v2:
time: 102 us
  Pallas kernels  97.7 us (96%)
  local copies, waits for them, and re-layouts  3.24 us (3%)
    pallas_call x1, Pallas kernels, local_terms(): pl.pallas_call(local_kernel, out_shape=jax.ShapeDtypeStruct((2, DEVICES /...  56.5 us
    pallas_call x1, Pallas kernels, combine(): pl.pallas_call(combine_kernel, out_shape=(jax.ShapeDtypeStruct((CLASSES *...  41.3 us
    unnamed x4, local copies, waits for them, and re-layouts  3.24 us

profile of v2, /device:TPU:1, one launch (start us, length us, event | category | flops | bytes accessed | tf_op | source)
XLA Modules:
  0.0 101.6 jit_solution(1883445526536642533)
XLA Ops:
  0.6 56.5 %local_terms.1.packed = bf16[2,64,32,128]{3,2,1,0:T(8,128)(2,1)} custom-call(s32[2,4,64]{2,1,0:T(4,128)} %pos.1, s32[4]{0:T(128)} %counts.1, bf16[4,1024,1024]{2,1,0:T(8,128)(2,1)} %mic.1, s32[4,64]{1,0:T(4,128)} %dest.1, f32[1,4096]{1,0:T(1,128)} %constant.4.clone.ys, f32[1,4096]{1,0:T(1,128)} %constant.5.clone.xs, bf16[100,32,128]{2,1,0:T(8,128)(2,1)} %tmpl.1), custom_call_target="tpu_custom_call" | custom-call | tf_op jit(solution)/shard_map/local_terms/pallas_call | solution.py:287
  57.1 41.3 %combine.1 = (f32[3200,128]{1,0:T(8,128)}, f32[1,128]{1,0:T(1,128)}) custom-call(bf16[2,64,32,128]{3,2,1,0:T(8,128)(2,1)} %local_terms.1.packed), custom_call_target="tpu_custom_call" | custom-call | tf_op jit(solution)/shard_map/combine/pallas_call | solution.py:450
  98.4 0.0 copy-start
  98.4 2.7 %copy.11 = f32[100,32,128]{2,1,0:T(8,128)} copy(f32[100,32,128]{2,1,0:T(8,128)} %bitcast.2) | data formatting | bytes 3276800
  101.1 0.0 copy-done
  101.1 0.5 copy.12
Async XLA Ops:
  98.4 2.7 %copy-start = (f32[1,128]{1,0:T(1,128)S(1)}, f32[1,128]{1,0:T(1,128)}, u32[]{:S(2)}) copy-start(f32[1,128]{1,0:T(1,128)} %get-tuple-element.5) | copy-start | bytes 1540

commit v3 on v2

v3 whole, which is shorter than its diff:
```python
import functools
import numpy as np
import jax
import jax.numpy as jnp
from jax import lax
from jax.experimental import pallas as pl
from jax.experimental.pallas import tpu as pltpu

BOX = 64
RAD = 32
ANG = 128
CLASSES = 100
ROTS = 36
CPAD = 104
QROT = 4
BASE = 9
NROWS = 4 * 2 * CPAD + 112
DEVICES = 128
CHIPS = DEVICES // 2
PIECE = 32
F32 = jnp.float32
BF16 = jnp.bfloat16


def sample_points():
    center = np.float32((BOX - 1) / 2.0)
    radius = (np.arange(RAD, dtype=np.float32) + np.float32(0.5)) * np.float32(BOX / 2.0 - 1.0) / np.float32(RAD)
    theta = np.float32(2.0 * np.pi) * np.arange(ANG, dtype=np.float32) / np.float32(ANG)
    ys = (center + radius[:, None] * np.sin(theta)[None, :]).reshape(1, -1)
    xs = (center + radius[:, None] * np.cos(theta)[None, :]).reshape(1, -1)
    def ordered(v):
        v = v.astype(np.float32).reshape(RAD // 4, 2, 2, 2, ANG // 2)
        v = v.transpose(0, 3, 1, 2, 4)
        v = np.stack([v[:, 0], v[:, 1, :, ::-1]], axis=1)
        return v.reshape(1, -1)

    return ordered(ys), ordered(xs)


def rotation_taps():
    a = np.arange(ANG, dtype=np.float32)
    taps = []
    for k in range(BASE):
        shift = np.float32(k) * np.float32(ANG) / np.float32(ROTS)
        d = a - np.float32(0) - shift
        d = d - ANG * np.floor(d / np.float32(ANG) + np.float32(0.5))
        w = np.maximum(np.float32(0), np.float32(1) - np.abs(d)).astype(jnp.bfloat16).astype(np.float32)
        first = int(32 * k // 9)
        taps.append((first, float(w[first]), float(w[(first + 1) % ANG]) if k else 0.0))
    return taps


TAPS = rotation_taps()


def turned_rows(x, i):
    if i == 8:
        return x[8 * CPAD : 9 * CPAD]
    pair = x[(i // 2) * 2 * CPAD : (i // 2 + 1) * 2 * CPAD].reshape(CPAD // 8, 16, x.shape[1])
    return pair[:, 8 * (i % 2) : 8 * (i % 2) + 8].reshape(CPAD, x.shape[1])


def remote(src, dst, send_sem, recv_sem, device):
    return pltpu.make_async_remote_copy(
        src_ref=src,
        dst_ref=dst,
        send_sem=send_sem,
        recv_sem=recv_sem,
        device_id=(device,),
        device_id_type=pl.DeviceIdType.MESH,
    )


def iteration_kernel(pos, counts, mic, dest, ys, xs, tmpl, means, evidence, extra, raw, planes, flat, boxes, wtile, tflat, byrad, rmat, rot, esum, shifted, scores, weights, tsum, sums_a, sums_b, out, half, send, landed, gathered, crossed, sems,
                     half_send, half_recv, put_send, put_recv, get_send, get_recv, cross_send, cross_recv):
    mics = mic.shape[0]
    slots = pos.shape[2]
    parts = mics * slots

    me = lax.axis_index("dev")
    core = lax.rem(me, 2)
    chip = me // 2
    partner = me + 1 - 2 * core

    barrier = pltpu.get_barrier_semaphore()
    pl.semaphore_signal(barrier, inc=1, device_id=(partner,), device_id_type=pl.DeviceIdType.MESH)

    def greet(k, _):
        pl.semaphore_signal(
            barrier, inc=1, device_id=(2 * (chip ^ k) + core,), device_id_type=pl.DeviceIdType.MESH
        )
        return 0

    lax.fori_loop(1, CHIPS, greet, 0)

    def fetch(i):
        return pltpu.make_async_copy(mic.at[i], raw.at[i % 2], sems.at[i % 2])

    fetch(0).start()
    fetch(1).start()

    lane1 = lax.broadcasted_iota(jnp.int32, (1, ANG), 1)

    away = lax.broadcasted_iota(jnp.int32, (ANG, ANG), 1) - lax.broadcasted_iota(jnp.int32, (ANG, ANG), 0)
    for i, (first, w0, w1) in enumerate(TAPS):
        step = (away - first) & 127
        turn = jnp.where(step == 0, w0, jnp.where(step == 1, w1, 0.0))
        rmat[:, i * ANG : (i + 1) * ANG] = turn.astype(BF16)
    tflat[pl.ds(CLASSES * RAD, (CPAD - CLASSES) * RAD), :] = jnp.zeros(((CPAD - CLASSES) * RAD, ANG), F32)
    tflat[pl.ds(0, CLASSES * RAD), :] = tmpl[...].reshape(CLASSES * RAD, ANG).astype(F32)
    esum[...] = jnp.zeros_like(esum)
    tiles = CPAD // 8

    def regroup(n, _):
        pair = [tflat[pl.ds(2 * n + h, CPAD, stride=RAD), :] for h in range(2)]
        byrad[pl.ds(pl.multiple_of(n * 2 * CPAD, 16), 2 * CPAD), :] = jnp.concatenate(pair, axis=0).astype(BF16)
        return 0

    lax.fori_loop(0, RAD // 2, regroup, 0, unroll=2)

    def rotate_block(n, _):
        few = 4
        block = byrad[pl.ds(pl.multiple_of(n * few * CPAD, 16), few * CPAD), :]
        for k in range(5):
            start, height = (k * 2 * CPAD, 2 * CPAD) if k < 4 else (8 * CPAD, 112)
            wide = jnp.dot(block, rmat[:, k * 2 * ANG : min(k * 2 + 2, 9) * ANG], preferred_element_type=F32)
            total = jnp.zeros((height, ANG), F32)
            for h in range(few):
                some = wide[h * CPAD : (h + 1) * CPAD]
                if k < 4:
                    some = [some[:, m * ANG : (m + 1) * ANG].reshape(tiles, 8, ANG) for m in range(2)]
                    some = jnp.concatenate(some, axis=1).reshape(2 * CPAD, ANG)
                else:
                    some = jnp.concatenate([some, jnp.zeros((8, ANG), F32)], axis=0)
                some = some.astype(BF16)
                col = pl.ds(pl.multiple_of((n * few + h) * ANG, ANG), ANG)
                rot[start : start + height, col] = some
                some = some.astype(F32)
                total += some * some
            esum[start : start + height, :] += total
        return 0

    lax.fori_loop(0, RAD // 4, rotate_block, 0)

    lanes = lax.broadcasted_iota(jnp.int32, (BOX // 2, ANG), 1)
    for i in range(mics):
        fetch(i).wait()
        for t in range(8):
            planes[t, :, :] = raw[i % 2, :, t * ANG : (t + 1) * ANG].astype(F32)
        if i + 2 < mics:
            fetch(i + 2).start()

        def cut(j, _, i=i):
            y = pos[0, i, j]
            x = pos[1, i, j]
            t = x >> 7
            s = x & 127
            t1 = jnp.minimum(t + 1, 7)
            even = pl.ds(y, BOX // 2, stride=2)
            odd = pl.ds(y + 1, BOX // 2, stride=2)
            keep = lanes >= s
            e = jnp.where(keep, planes[t, even, :], planes[t1, even, :])
            o = jnp.where(keep, planes[t, odd, :], planes[t1, odd, :])
            e = pltpu.roll(e, (ANG - s) & 127, 1)
            o = pltpu.roll(o, (ANG + BOX - s) & 127, 1)
            flat[pl.ds(pl.multiple_of((i * slots + j) * (BOX // 2), BOX // 2), BOX // 2), :] = jnp.where(lanes < BOX, e, o)
            return 0

        lax.fori_loop(0, slots, cut, 0, unroll=8)

    for s in range(BOX // 2):
        boxes[:, s * ANG : (s + 1) * ANG] = flat[pl.ds(s, parts, stride=BOX // 2), :].astype(BF16)

    pix = lax.broadcasted_iota(jnp.int32, (BOX, 2 * ANG), 0).astype(F32)
    left = lax.broadcasted_iota(jnp.int32, (parts, ANG), 1) < BOX
    for g in range(RAD // 4):
        radius = (4 * g + 3.5) * (BOX / 2.0 - 1.0) / RAD
        reach = (int(np.floor(31.501 + radius)) + 3) // 2 * 2
        halves = []
        for side in range(2):
            low, high = (30, reach) if side == 0 else (BOX - reach, 34)
            cols = slice((2 * g + side) * 2 * ANG, (2 * g + side + 1) * 2 * ANG)
            rw = jnp.maximum(0.0, 1.0 - jnp.abs(pix - ys[:, cols]))
            cw = jnp.maximum(0.0, 1.0 - jnp.abs(pix - xs[:, cols]))
            w = wtile.at[side]
            for u in range(low, high):
                w[(u - low) * BOX : (u - low + 1) * BOX, :] = (rw[u : u + 1, :] * cw).astype(BF16)
            halves.append(
                jnp.dot(
                    boxes[:, low * BOX : high * BOX],
                    w[: (high - low) * BOX, :],
                    preferred_element_type=F32,
                )
            )
        for m in range(2):
            upper = halves[0][:, m * ANG : (m + 1) * ANG]
            lower = halves[1][:, m * ANG : (m + 1) * ANG]
            for h in range(2):
                whole = jnp.where(left, upper, lower) if h == 0 else jnp.where(left, lower, upper)
                c0 = (4 * g + 2 * m + h) * ANG
                for j in range(QROT):
                    turn = (BOX * h - 32 * j) % ANG
                    part = pltpu.roll(whole, turn, 1) if turn else whole
                    shifted[j * parts : (j + 1) * parts, c0 : c0 + ANG] = part.astype(BF16)

    rows = lax.broadcasted_iota(jnp.int32, (NROWS, 1), 0)
    energy = 0.5 * jnp.sum(esum[...], axis=1, keepdims=True)
    paired = lax.rem(rows >> 4, 13) * 8 + (rows & 7)
    pad = jnp.where(rows < 8 * CPAD, paired, rows - 8 * CPAD) >= CLASSES
    energy = jnp.where(pad, 1e30, energy)

    def score(j, peak):
        rows_j = pl.ds(pl.multiple_of(j * parts, parts), parts)
        prod = lax.dot_general(rot[...], shifted[rows_j, :], (((1,), (1,)), ((), ())), preferred_element_type=F32)
        prod = prod - energy
        scores[:, rows_j] = prod
        return jnp.maximum(peak, jnp.max(prod, axis=0, keepdims=True))

    peak = lax.fori_loop(0, QROT, score, jnp.full((1, parts), -3e38, F32))
    peak4 = jnp.concatenate([peak] * QROT, axis=1)

    def expo(n, acc):
        rr = pl.ds(pl.multiple_of(n * 16, 16), 16)
        e = jnp.exp(scores[rr, :] - peak4)
        scores[rr, :] = e
        return acc + e[:8] + e[8:]

    acc = lax.fori_loop(0, NROWS // 16, expo, jnp.zeros((8, QROT * parts), F32))
    norm = jnp.sum(acc, axis=0, keepdims=True)
    norm = sum(norm[:, j * parts : (j + 1) * parts] for j in range(QROT))
    loglik = peak + jnp.log(norm)

    lane = lax.broadcasted_iota(jnp.int32, (1, parts), 1)
    target = jnp.concatenate([dest[i : i + 1, :] for i in range(mics)], axis=1)
    live = target >= 0
    for i in range(mics):
        live = live & ((lane < i * slots + counts[i]) | (lane >= (i + 1) * slots))
    inv = jnp.where(live, 1.0 / norm, 0.0)
    inv4 = jnp.concatenate([inv] * QROT, axis=1)

    def weigh(n, _):
        rr = pl.ds(pl.multiple_of(n * 16, 16), 16)
        w = (scores[rr, :] * inv4).astype(BF16)
        weights[rr, :] = w
        wide = w.astype(F32)
        tsum[rr, :] = sum(wide[:, k * ANG : (k + 1) * ANG] for k in range(QROT * parts // ANG))
        return 0

    lax.fori_loop(0, NROWS // 16, weigh, 0)
    tot = jnp.sum(sum(turned_rows(tsum[...], i) for i in range(BASE)), axis=1, keepdims=True)
    spot = lax.broadcasted_iota(jnp.int32, (CPAD, ANG), 0) == lax.broadcasted_iota(jnp.int32, (CPAD, ANG), 1)
    tot = jnp.sum(jnp.where(spot, tot, 0.0), axis=0, keepdims=True)
    high = tot.astype(BF16).astype(F32)
    first = core == 0
    extra[...] = jnp.zeros_like(extra)
    for value, here, there in ((high, 1, 6), (tot - high, 2, 7)):
        value = jnp.broadcast_to(value, (DEVICES, ANG))
        extra[pl.ds(here, DEVICES, stride=8), :] = jnp.where(first, value, 0.0)
        extra[pl.ds(there, DEVICES, stride=8), :] = jnp.where(first, 0.0, value)

    which = lax.broadcasted_iota(jnp.int32, (ANG, parts), 0)
    owner = jnp.where((which == (target >> 7)) & live, 1.0, 0.0)
    row = jnp.where(which == (target & 127), 1.0, 0.0).astype(BF16)
    rest = loglik
    for k in range(3):
        piece = rest.astype(BF16).astype(F32)
        table = lax.dot_general((owner * piece).astype(BF16), row, (((1,), (1,)), ((), ())), preferred_element_type=F32)
        extra[pl.ds(3 + k, DEVICES, stride=8), :] = table
        rest = rest - piece

    top = lax.broadcasted_iota(jnp.int32, (8, ANG), 0)

    def turn(n):
        return n ^ (chip // 4)

    def product(n, into):
        g = turn(n)
        cols = pl.ds(pl.multiple_of(g * 2 * ANG, 2 * ANG), 2 * ANG)
        into[...] = jnp.dot(weights[...], shifted[:, cols], preferred_element_type=F32)

    def fold(n, source):
        g = turn(n)
        for k in range(2):
            sum0 = jnp.zeros((CPAD, ANG), F32)
            sum1 = jnp.zeros((CPAD, ANG), F32)
            half = source[:, k * ANG : (k + 1) * ANG]
            for i, (first, w0, w1) in enumerate(TAPS):
                q = turned_rows(half, i)
                if first:
                    q = pltpu.roll(q, ANG - first, 1)
                sum0 += w0 * q
                if w1:
                    sum1 += w1 * q
            total = sum0 + pltpu.roll(sum1, ANG - 1, 1)
            r = 2 * g + k
            for q in range(4):
                tail = total[96:] if q == 0 else pltpu.roll(total[96:], 8 - q, 0)
                spare = extra[pl.ds(pl.multiple_of((4 * r + q) * 8, 8), 8), :]
                tail = jnp.where(top == 0, tail, spare)
                piece = jnp.concatenate([total[24 * q : 24 * q + 24], tail], axis=0)
                out[q % 2, 2 * r + q // 2, :, :] = piece.astype(BF16)

    def half_copy(n):
        at = pl.ds(4 * turn(n), 4)
        return remote(out.at[1 - core, at], half.at[at], half_send.at[n], half_recv.at[n], partner)

    def put(c, slot):
        return remote(send.at[c], landed.at[slot], put_send.at[c], put_recv.at[slot], 2 * c + core)

    def give(n):
        half_copy(n).wait_recv()
        for m in range(4):
            c = 4 * turn(n) + m
            send[c] = (out[core, c].astype(F32) + half[c].astype(F32)).astype(BF16)
        for m in range(4):
            c = 4 * turn(n) + m

            @pl.when(c != chip)
            def _():
                put(c, chip).start()

    product(0, sums_a)
    pl.semaphore_wait(barrier, CHIPS)

    def step(n, now, later):
        @pl.when(n >= 2)
        def _():
            give(n - 2)

        product(n + 1, later)
        fold(n, now)
        half_copy(n).start()

    def collect(n, _):
        step(2 * n, sums_a, sums_b)
        step(2 * n + 1, sums_b, sums_a)
        return 0

    last = RAD // 2 - 1
    lax.fori_loop(0, last // 2, collect, 0)
    give(last - 3)
    product(last, sums_b)
    fold(last - 1, sums_a)
    half_copy(last - 1).start()
    fold(last, sums_b)
    half_copy(last).start()
    for n in (last - 2, last - 1, last):
        give(n)

    def take(k, acc):
        c = chip ^ k
        remote(send.at[c], landed.at[c], put_send.at[c], put_recv.at[c], 2 * c + core).wait_recv()
        return acc + landed[c].astype(F32)

    acc = lax.fori_loop(1, CHIPS, take, send[chip].astype(F32))

    quarter = 2 * lax.rem(chip, 2) + core
    row = lax.broadcasted_iota(jnp.int32, (PIECE, ANG), 0)
    lane = lax.broadcasted_iota(jnp.int32, (PIECE, ANG), 1)
    which = jnp.where(row < 24, 24 * quarter + row, 96 + quarter)
    total = acc[25:26] + acc[26:27] + acc[30:31] + acc[31:32]
    total = jnp.sum(jnp.where(lane == which, total, 0.0), axis=1, keepdims=True)
    gathered[chip] = (acc / jnp.maximum(total, 1.0)).astype(BF16)
    evidence[...] = acc[27:28] + acc[28:29] + acc[29:30]

    def share(c, to):
        return remote(gathered.at[c], gathered.at[c], get_send.at[to], get_recv.at[c], 2 * to + core)

    def pass_on(c):
        return remote(gathered.at[c], crossed.at[c], cross_send.at[c], cross_recv.at[c], partner)

    def spread(k, _):
        share(chip, chip ^ k).start()
        return 0

    lax.fori_loop(1, CHIPS, spread, 0)
    pass_on(chip).start()

    def write(piece, c, k):
        r = c // 2
        q = 2 * lax.rem(c, 2) + k
        wide = piece.astype(F32)
        means[pl.ds(24 * RAD * q + r, 24, stride=RAD), :] = wide[:24]
        means[pl.ds((96 + q) * RAD + r, 1), :] = wide[24:25]

    write(gathered[chip], chip, core)

    def pick(k, _):
        c = chip ^ k
        share(c, c).wait_recv()
        pass_on(c).start()
        write(gathered[c], c, core)
        return 0

    lax.fori_loop(1, CHIPS, pick, 0)

    def cross(k, _):
        c = chip ^ k
        pass_on(c).wait_recv()
        write(crossed[c], c, 1 - core)
        return 0

    lax.fori_loop(0, CHIPS, cross, 0)

    def drain_half(n, _):
        half_copy(n).wait_send()
        return 0

    lax.fori_loop(0, RAD // 2, drain_half, 0)
    def drain(k, _):
        c = chip ^ k
        put(c, chip).wait_send()
        share(chip, c).wait_send()
        pass_on(c).wait_send()
        return 0

    lax.fori_loop(1, CHIPS, drain, 0)
    pass_on(chip).wait_send()


def iteration(micrographs, positions, counts, dest_rows, templates):
    mics, slots = dest_rows.shape
    parts = mics * slots
    cells = RAD * ANG
    ys, xs = sample_points()
    vmem = pl.BlockSpec(memory_space=pltpu.VMEM)
    smem = pl.BlockSpec(memory_space=pltpu.SMEM)
    return pl.pallas_call(
        iteration_kernel,
        out_shape=(
            jax.ShapeDtypeStruct((CLASSES * RAD, ANG), F32),
            jax.ShapeDtypeStruct((1, ANG), F32),
        ),
        in_specs=[smem, smem, pl.BlockSpec(memory_space=pl.ANY), vmem, vmem, vmem, vmem],
        out_specs=(vmem, vmem),
        scratch_shapes=[
            pltpu.VMEM((DEVICES * 8, ANG), F32),
            pltpu.VMEM((2, 1024, 1024), BF16),
            pltpu.VMEM((8, 1024, ANG), F32),
            pltpu.VMEM((BOX // 2 * parts, ANG), F32),
            pltpu.VMEM((parts, BOX * BOX), BF16),
            pltpu.VMEM((2, 34 * BOX, 2 * ANG), BF16),
            pltpu.VMEM((CPAD * RAD, ANG), F32),
            pltpu.VMEM((CPAD * RAD, ANG), BF16),
            pltpu.VMEM((ANG, BASE * ANG), BF16),
            pltpu.VMEM((NROWS, cells), BF16),
            pltpu.VMEM((NROWS, ANG), F32),
            pltpu.VMEM((QROT * parts, cells), BF16),
            pltpu.VMEM((NROWS, QROT * parts), F32),
            pltpu.VMEM((NROWS, QROT * parts), BF16),
            pltpu.VMEM((NROWS, ANG), F32),
            pltpu.VMEM((NROWS, 2 * ANG), F32),
            pltpu.VMEM((NROWS, 2 * ANG), F32),
            pltpu.VMEM((2, CHIPS, PIECE, ANG), BF16),
        ]
        + [pltpu.VMEM((CHIPS, PIECE, ANG), BF16)] * 5
        + [pltpu.SemaphoreType.DMA((n,)) for n in (2, 16, 16, 64, 64, 64, 64, 64, 64)],
        compiler_params=pltpu.CompilerParams(
            vmem_limit_bytes=60 * 1024 * 1024, collective_id=0, has_side_effects=True
        ),
        name="iteration",
    )(positions, counts, micrographs, dest_rows, jnp.asarray(ys), jnp.asarray(xs), templates)
def on_device(micrographs, positions, counts, dest_rows, templates):
    means, loglik = iteration(micrographs, positions, counts, dest_rows, templates)
    return means.reshape(CLASSES, RAD, ANG), loglik.reshape(ANG)


def solution(mesh):
    P = jax.sharding.PartitionSpec
    return jax.shard_map(
        on_device,
        mesh=mesh,
        in_specs=(P("dev", None, None), P(None, "dev", None), P("dev"), P("dev", None), P()),
        out_specs=(P(), P("dev")),
        check_vma=False,
    )
```

time: 102 us -> 81.8 us (0.80)
  Pallas kernels: 97.7 us -> 77.7 us
    pallas_call x2 -> x1, Pallas kernels: 97.7 us -> 77.7 us  [iteration(): pl.pallas_call(iteration_kernel, out_shape=(jax.ShapeDtypeStruct((CLASSES...]
where the time goes in v3:
time: 81.8 us; the launch traced here: 81.6 us
  Pallas kernels  77.7 us (95%)
  local copies, waits for them, and re-layouts  3.24 us (4%)
    pallas_call x1, Pallas kernels, iteration(): pl.pallas_call(iteration_kernel, out_shape=(jax.ShapeDtypeStruct((CLASSES...  77.7 us
    unnamed x4, local copies, waits for them, and re-layouts  3.24 us

profile of v3, /device:TPU:1, one launch (start us, length us, event | category | flops | bytes accessed | tf_op | source)
XLA Modules:
  0.0 81.6 jit_solution(14375404790044713408)
XLA Ops:
  0.6 77.7 %iteration.1 = (f32[3200,128]{1,0:T(8,128)}, f32[1,128]{1,0:T(1,128)}) custom-call(s32[2,4,64]{2,1,0:T(4,128)} %pos.1, s32[4]{0:T(128)} %counts.1, bf16[4,1024,1024]{2,1,0:T(8,128)(2,1)} %mic.1, s32[4,64]{1,0:T(4,128)} %dest.1, f32[1,4096]{1,0:T(1,128)} %constant.4.clone.ys, f32[1,4096]{1,0:T(1,128)} %constant.5.clone.xs, bf16[100,32,128]{2,1,0:T(8,128)(2,1)} %tmpl.1), custom_call_target="tpu_custom_call" | custom-call | tf_op jit(solution)/shard_map/iteration/pallas_call | solution.py:428
  78.3 0.0 copy-start
  78.4 2.7 %copy.11 = f32[100,32,128]{2,1,0:T(8,128)} copy(f32[100,32,128]{2,1,0:T(8,128)} %bitcast.2) | data formatting | bytes 3276800
  81.1 0.0 copy-done
  81.1 0.5 copy.12
Async XLA Ops:
  78.3 2.7 %copy-start = (f32[1,128]{1,0:T(1,128)S(1)}, f32[1,128]{1,0:T(1,128)}, u32[]{:S(2)}) copy-start(f32[1,128]{1,0:T(1,128)} %get-tuple-element.5) | copy-start | bytes 1540

commit v4 on v3

--- a/solution.py
+++ b/solution.py
@@ -71,7 +71,7 @@
     )
 
 
-def iteration_kernel(pos, counts, mic, dest, ys, xs, tmpl, means, evidence, extra, raw, planes, flat, boxes, wtile, tflat, byrad, rmat, rot, esum, shifted, scores, weights, tsum, sums_a, sums_b, out, half, send, landed, gathered, crossed, sems,
+def iteration_kernel(pos, counts, mic, dest, ys, xs, tmpl, means, evidence, extra, raw, planes, flat, boxes, wtile, tflat, byrad, rmat, rot, esum, shifted, scores, weights, tsum, sums_a, sums_b, out, half, send, landed, gathered, crossed, table, sems,
                      half_send, half_recv, put_send, put_recv, get_send, get_recv, cross_send, cross_recv):
     mics = mic.shape[0]
     slots = pos.shape[2]
@@ -264,8 +264,8 @@
     rest = loglik
     for k in range(3):
         piece = rest.astype(BF16).astype(F32)
-        table = lax.dot_general((owner * piece).astype(BF16), row, (((1,), (1,)), ((), ())), preferred_element_type=F32)
-        extra[pl.ds(3 + k, DEVICES, stride=8), :] = table
+        placed = lax.dot_general((owner * piece).astype(BF16), row, (((1,), (1,)), ((), ())), preferred_element_type=F32)
+        extra[pl.ds(3 + k, DEVICES, stride=8), :] = placed
         rest = rest - piece
 
     top = lax.broadcasted_iota(jnp.int32, (8, ANG), 0)
@@ -302,57 +302,71 @@
 
     def half_copy(n):
         at = pl.ds(4 * turn(n), 4)
-        return remote(out.at[1 - core, at], half.at[at], half_send.at[n], half_recv.at[n], partner)
-
-    def put(c, slot):
-        return remote(send.at[c], landed.at[slot], put_send.at[c], put_recv.at[slot], 2 * c + core)
-
-    def give(n):
+        return remote(out.at[1 - core, at], half.at[at], half_send, half_recv.at[n], partner)
+
+    def put(c):
+        return remote(send.at[c], landed.at[chip], put_send, put_recv, 2 * c + core)
+
+    def give(n, home=False):
         half_copy(n).wait_recv()
         for m in range(4):
             c = 4 * turn(n) + m
             send[c] = (out[core, c].astype(F32) + half[c].astype(F32)).astype(BF16)
+        if home:
+            landed[chip] = send[chip]
         for m in range(4):
             c = 4 * turn(n) + m
-
-            @pl.when(c != chip)
-            def _():
-                put(c, chip).start()
-
+            if home:
+
+                @pl.when(c != chip)
+                def _():
+                    put(c).start()
+
+            else:
+                put(c).start()
+
+    def pair(n):
+        product(2 * n + 1, sums_b)
+        fold(2 * n, sums_a)
+        product(2 * n + 2, sums_a)
+        fold(2 * n + 1, sums_b)
+        half_copy(2 * n).start()
+        half_copy(2 * n + 1).start()
+
+    def alone(n, _):
+        pair(n)
+        return 0
+
+    def sending(n, _):
+        pair(n)
+        give(2 * n - 2)
+        give(2 * n - 1)
+        return 0
+
+    last = RAD // 2 - 1
     product(0, sums_a)
     pl.semaphore_wait(barrier, CHIPS)
-
-    def step(n, now, later):
-        @pl.when(n >= 2)
-        def _():
-            give(n - 2)
-
-        product(n + 1, later)
-        fold(n, now)
-        half_copy(n).start()
-
-    def collect(n, _):
-        step(2 * n, sums_a, sums_b)
-        step(2 * n + 1, sums_b, sums_a)
-        return 0
-
-    last = RAD // 2 - 1
-    lax.fori_loop(0, last // 2, collect, 0)
-    give(last - 3)
+    lax.fori_loop(0, 2, alone, 0)
+    give(0, home=True)
+    give(1)
+    lax.fori_loop(2, last // 2, sending, 0)
     product(last, sums_b)
     fold(last - 1, sums_a)
     half_copy(last - 1).start()
+    give(last - 3)
+    give(last - 2)
     fold(last, sums_b)
     half_copy(last).start()
-    for n in (last - 2, last - 1, last):
-        give(n)
+    give(last - 1)
+    give(last)
+
+    others = pl.ds(0, CHIPS - 1)
+    remote(send.at[others], landed.at[others], put_send, put_recv, partner).wait_recv()
 
     def take(k, acc):
-        c = chip ^ k
-        remote(send.at[c], landed.at[c], put_send.at[c], put_recv.at[c], 2 * c + core).wait_recv()
-        return acc + landed[c].astype(F32)
-
-    acc = lax.fori_loop(1, CHIPS, take, send[chip].astype(F32))
+        return acc + sum(landed[8 * k + m].astype(F32) for m in range(8))
+
+    acc = lax.fori_loop(0, CHIPS // 8, take, jnp.zeros((PIECE, ANG), F32))
 
     quarter = 2 * lax.rem(chip, 2) + core
     row = lax.broadcasted_iota(jnp.int32, (PIECE, ANG), 0)
@@ -363,59 +377,62 @@
     gathered[chip] = (acc / jnp.maximum(total, 1.0)).astype(BF16)
     evidence[...] = acc[27:28] + acc[28:29] + acc[29:30]
 
-    def share(c, to):
-        return remote(gathered.at[c], gathered.at[c], get_send.at[to], get_recv.at[c], 2 * to + core)
+    def share(slot, to):
+        return remote(gathered.at[slot], gathered.at[slot], get_send, get_recv.at[slot], 2 * to + core)
 
     def pass_on(c):
-        return remote(gathered.at[c], crossed.at[c], cross_send.at[c], cross_recv.at[c], partner)
+        return remote(gathered.at[c], crossed.at[c], cross_send, cross_recv.at[c], partner)
 
     def spread(k, _):
         share(chip, chip ^ k).start()
         return 0
 
-    lax.fori_loop(1, CHIPS, spread, 0)
+    lax.fori_loop(1, CHIPS, spread, 0, unroll=3)
     pass_on(chip).start()
 
     def write(piece, c, k):
         r = c // 2
         q = 2 * lax.rem(c, 2) + k
         wide = piece.astype(F32)
-        means[pl.ds(24 * RAD * q + r, 24, stride=RAD), :] = wide[:24]
-        means[pl.ds((96 + q) * RAD + r, 1), :] = wide[24:25]
-
-    write(gathered[chip], chip, core)
-
-    def pick(k, _):
+        table[pl.ds(24 * RAD * q + r, 24, stride=RAD), :] = wide[:24]
+        table[pl.ds((96 + q) * RAD + r, 1), :] = wide[24:25]
+
+    def cross(k):
+        c = chip ^ k
+        pass_on(c).wait_recv()
+        write(crossed[c], c, 1 - core)
+
+    def pick(k):
         c = chip ^ k
         share(c, c).wait_recv()
         pass_on(c).start()
         write(gathered[c], c, core)
-        return 0
-
-    lax.fori_loop(1, CHIPS, pick, 0)
-
-    def cross(k, _):
-        c = chip ^ k
-        pass_on(c).wait_recv()
-        write(crossed[c], c, 1 - core)
-        return 0
-
-    lax.fori_loop(0, CHIPS, cross, 0)
-
-    def drain_half(n, _):
-        half_copy(n).wait_send()
-        return 0
-
-    lax.fori_loop(0, RAD // 2, drain_half, 0)
-    def drain(k, _):
-        c = chip ^ k
-        put(c, chip).wait_send()
-        share(chip, c).wait_send()
-        pass_on(c).wait_send()
-        return 0
-
-    lax.fori_loop(1, CHIPS, drain, 0)
-    pass_on(chip).wait_send()
+
+    lag = 6
+    write(gathered[chip], chip, core)
+
+    def early(k, _):
+        pick(k)
+        return 0
+
+    def both(k, _):
+        pick(k)
+        cross(k - lag)
+        return 0
+
+    def late(k, _):
+        cross(k)
+        return 0
+
+    lax.fori_loop(1, lag, early, 0)
+    lax.fori_loop(lag, CHIPS, both, 0)
+    lax.fori_loop(CHIPS - lag, CHIPS, late, 0)
+    means[...] = table[...].astype(BF16)
+
+    remote(out.at[1 - core], half, half_send, half_recv.at[0], partner).wait_send()
+    remote(send.at[others], landed.at[others], put_send, put_recv, partner).wait_send()
+    remote(gathered.at[others], landed.at[others], get_send, put_recv, partner).wait_send()
+    remote(gathered, crossed, cross_send, put_recv, partner).wait_send()
 
 
 def iteration(micrographs, positions, counts, dest_rows, templates):
@@ -425,10 +442,12 @@
     ys, xs = sample_points()
     vmem = pl.BlockSpec(memory_space=pltpu.VMEM)
     smem = pl.BlockSpec(memory_space=pltpu.SMEM)
+    one = pltpu.SemaphoreType.DMA
+    many = pltpu.SemaphoreType.DMA((CHIPS,))
     return pl.pallas_call(
         iteration_kernel,
         out_shape=(
-            jax.ShapeDtypeStruct((CLASSES * RAD, ANG), F32),
+            jax.ShapeDtypeStruct((CLASSES * RAD, ANG), BF16),
             jax.ShapeDtypeStruct((1, ANG), F32),
         ),
         in_specs=[smem, smem, pl.BlockSpec(memory_space=pl.ANY), vmem, vmem, vmem, vmem],
@@ -454,7 +473,8 @@
             pltpu.VMEM((2, CHIPS, PIECE, ANG), BF16),
         ]
         + [pltpu.VMEM((CHIPS, PIECE, ANG), BF16)] * 5
-        + [pltpu.SemaphoreType.DMA((n,)) for n in (2, 16, 16, 64, 64, 64, 64, 64, 64)],
+        + [pltpu.VMEM((CLASSES * RAD, ANG), F32), pltpu.SemaphoreType.DMA((2,))]
+        + [one, pltpu.SemaphoreType.DMA((RAD // 2,)), one, one, one, many, one, many],
         compiler_params=pltpu.CompilerParams(
             vmem_limit_bytes=60 * 1024 * 1024, collective_id=0, has_side_effects=True
         ),
@@ -462,7 +482,7 @@
     )(positions, counts, micrographs, dest_rows, jnp.asarray(ys), jnp.asarray(xs), templates)
 def on_device(micrographs, positions, counts, dest_rows, templates):
     means, loglik = iteration(micrographs, positions, counts, dest_rows, templates)
-    return means.reshape(CLASSES, RAD, ANG), loglik.reshape(ANG)
+    return means.reshape(CLASSES, RAD, ANG).astype(F32), loglik.reshape(ANG)
 
 
 def solution(mesh):

time: 81.8 us -> 76.5 us (0.935)
  Pallas kernels: 77.7 us -> 71.6 us
  other arithmetic: 0 us -> 2.54 us
  local copies, waits for them, and re-layouts: 3.24 us -> 1.18 us
    pallas_call x1, Pallas kernels: 77.7 us -> 71.6 us  [iteration(): pl.pallas_call(iteration_kernel, out_shape=(jax.ShapeDtypeStruct((CLASSES...]
    convert_element_type x0 -> x1, other arithmetic: none -> 2.54 us  [on_device(): return (means.reshape(CLASSES, RAD, ANG).astype(F32), loglik.reshape(ANG))]
    unnamed x4 -> x1, local copies, waits for them, and re-layouts: 3.24 us -> 1.18 us
where the time goes in v4:
time: 76.5 us; the launch traced here: 76 us
  Pallas kernels  71.6 us (94%)
  other arithmetic  2.54 us (3%)
  local copies, waits for them, and re-layouts  1.18 us (2%)
    pallas_call x1, Pallas kernels, iteration(): pl.pallas_call(iteration_kernel, out_shape=(jax.ShapeDtypeStruct((CLASSES...  71.6 us
    convert_element_type x1, other arithmetic, on_device(): return (means.reshape(CLASSES, RAD, ANG).astype(F32), loglik.reshape(ANG))  2.54 us

profile of v4, /device:TPU:1, one launch (start us, length us, event | category | flops | bytes accessed | tf_op | source)
XLA Modules:
  0.0 76.0 jit_solution(1835836222170568028)
XLA Ops:
  0.6 71.6 %iteration.1 = (bf16[3200,128]{1,0:T(8,128)(2,1)}, f32[1,128]{1,0:T(1,128)}) custom-call(s32[2,4,64]{2,1,0:T(4,128)} %pos.1, s32[4]{0:T(128)} %counts.1, bf16[4,1024,1024]{2,1,0:T(8,128)(2,1)} %mic.1, s32[4,64]{1,0:T(4,128)} %dest.1, f32[1,4096]{1,0:T(1,128)} %constant.4.clone.ys, f32[1,4096]{1,0:T(1,128)} %constant.5.clone.xs, bf16[100,32,128]{2,1,0:T(8,128)(2,1)} %tmpl.1), custom_call_target="tpu_custom_call" | custom-call | tf_op jit(solution)/shard_map/iteration/pallas_call | solution.py:447
  72.2 2.5 %convert.1 = f32[100,32,128]{2,1,0:T(8,128)} convert(bf16[100,32,128]{2,1,0:T(8,128)(2,1)} %bitcast.3) | non-fusion elementwise | flops 409600 | bytes 2457600 | tf_op jit(solution)/shard_map/convert_element_type | solution.py:485
  74.8 1.2 %copy.10 = f32[128]{0:T(128)} copy(f32[128]{0:T(128)} %bitcast.4) | data formatting | bytes 1024

commit v5 on v4

--- a/solution.py
+++ b/solution.py
@@ -225,7 +225,11 @@
         scores[rr, :] = e
         return acc + e[:8] + e[8:]
 
-    acc = lax.fori_loop(0, NROWS // 16, expo, jnp.zeros((8, QROT * parts), F32))
+    def expo_pair(n, acc):
+        return expo(2 * n + 1, expo(2 * n, acc))
+
+    acc = lax.fori_loop(0, NROWS // 32, expo_pair, jnp.zeros((8, QROT * parts), F32))
+    acc = expo(NROWS // 16 - 1, acc)
     norm = jnp.sum(acc, axis=0, keepdims=True)
     norm = sum(norm[:, j * parts : (j + 1) * parts] for j in range(QROT))
     loglik = peak + jnp.log(norm)
@@ -246,7 +250,12 @@
         tsum[rr, :] = sum(wide[:, k * ANG : (k + 1) * ANG] for k in range(QROT * parts // ANG))
         return 0
 
-    lax.fori_loop(0, NROWS // 16, weigh, 0)
+    def weigh_pair(n, _):
+        weigh(2 * n, 0)
+        return weigh(2 * n + 1, 0)
+
+    lax.fori_loop(0, NROWS // 32, weigh_pair, 0)
+    weigh(NROWS // 16 - 1, 0)
     tot = jnp.sum(sum(turned_rows(tsum[...], i) for i in range(BASE)), axis=1, keepdims=True)
     spot = lax.broadcasted_iota(jnp.int32, (CPAD, ANG), 0) == lax.broadcasted_iota(jnp.int32, (CPAD, ANG), 1)
     tot = jnp.sum(jnp.where(spot, tot, 0.0), axis=0, keepdims=True)
@@ -271,7 +280,7 @@
     top = lax.broadcasted_iota(jnp.int32, (8, ANG), 0)
 
     def turn(n):
-        return n ^ (chip // 4)
+        return (RAD // 2 - 1 - n) ^ (chip // 4)
 
     def product(n, into):
         g = turn(n)
@@ -347,7 +356,7 @@
     product(0, sums_a)
     pl.semaphore_wait(barrier, CHIPS)
     lax.fori_loop(0, 2, alone, 0)
-    give(0, home=True)
+    give(0)
     give(1)
     lax.fori_loop(2, last // 2, sending, 0)
     product(last, sums_b)
@@ -358,7 +367,7 @@
     fold(last, sums_b)
     half_copy(last).start()
     give(last - 1)
-    give(last)
+    give(last, home=True)
 
     others = pl.ds(0, CHIPS - 1)
     remote(send.at[others], landed.at[others], put_send, put_recv, partner).wait_recv()
@@ -384,10 +393,11 @@
         return remote(gathered.at[c], crossed.at[c], cross_send, cross_recv.at[c], partner)
 
     def spread(k, _):
-        share(chip, chip ^ k).start()
-        return 0
-
-    lax.fori_loop(1, CHIPS, spread, 0, unroll=3)
+        share(chip, chip ^ k ^ 42).start()
+        return 0
+
+    lax.fori_loop(0, 42, spread, 0, unroll=3)
+    lax.fori_loop(43, CHIPS, spread, 0, unroll=3)
     pass_on(chip).start()
 
     def write(piece, c, k):
@@ -480,9 +490,30 @@
         ),
         name="iteration",
     )(positions, counts, micrographs, dest_rows, jnp.asarray(ys), jnp.asarray(xs), templates)
+def widen_kernel(means, loglik, wide, same):
+    wide[...] = means[...].astype(F32)
+    same[...] = loglik[...]
+
+
+def widen(means, loglik):
+    rows = CLASSES * RAD // 4
+    return pl.pallas_call(
+        widen_kernel,
+        grid=(4,),
+        out_shape=(
+            jax.ShapeDtypeStruct((CLASSES * RAD, ANG), F32),
+            jax.ShapeDtypeStruct((1, ANG), F32),
+        ),
+        in_specs=[pl.BlockSpec((rows, ANG), lambda i: (i, 0)), pl.BlockSpec((1, ANG), lambda i: (0, 0))],
+        out_specs=(pl.BlockSpec((rows, ANG), lambda i: (i, 0)), pl.BlockSpec((1, ANG), lambda i: (0, 0))),
+        name="widen",
+    )(means, loglik)
+
+
 def on_device(micrographs, positions, counts, dest_rows, templates):
     means, loglik = iteration(micrographs, positions, counts, dest_rows, templates)
-    return means.reshape(CLASSES, RAD, ANG).astype(F32), loglik.reshape(ANG)
+    means, loglik = widen(means, loglik)
+    return means.reshape(CLASSES, RAD, ANG), loglik.reshape(ANG)
 
 
 def solution(mesh):

time: 76.5 us -> 75.8 us (level)
  Pallas kernels: 71.6 us -> 75 us
  other arithmetic: 2.54 us -> 0 us
  local copies, waits for them, and re-layouts: 1.18 us -> 0 us
    pallas_call x0 -> x1, Pallas kernels: none -> 3.46 us  [widen(): pl.pallas_call(widen_kernel, grid=(4,), out_shape=(jax.ShapeDtypeStruct((...]
    convert_element_type x1 -> x0, other arithmetic: 2.54 us -> none  [on_device(): return (means.reshape(CLASSES, RAD, ANG).astype(F32), loglik.reshape(ANG))]
    unnamed x1 -> x0, local copies, waits for them, and re-layouts: 1.18 us -> none
where the time goes in v5:
time: 75.8 us; the launch traced here: 75.6 us
  Pallas kernels  75 us (99%)
    pallas_call x1, Pallas kernels, iteration(): pl.pallas_call(iteration_kernel, out_shape=(jax.ShapeDtypeStruct((CLASSES...  71.5 us
    pallas_call x1, Pallas kernels, widen(): pl.pallas_call(widen_kernel, grid=(4,), out_shape=(jax.ShapeDtypeStruct((...  3.46 us

profile of v5, /device:TPU:1, one launch (start us, length us, event | category | flops | bytes accessed | tf_op | source)
XLA Modules:
  0.0 75.6 jit_solution(11271291427336285627)
XLA Ops:
  0.6 71.5 %iteration.1 = (bf16[3200,128]{1,0:T(8,128)(2,1)}, f32[1,128]{1,0:T(1,128)}) custom-call(s32[2,4,64]{2,1,0:T(4,128)} %pos.1, s32[4]{0:T(128)} %counts.1, bf16[4,1024,1024]{2,1,0:T(8,128)(2,1)} %mic.1, s32[4,64]{1,0:T(4,128)} %dest.1, f32[1,4096]{1,0:T(1,128)} %constant.4.clone.ys, f32[1,4096]{1,0:T(1,128)} %constant.5.clone.xs, bf16[100,32,128]{2,1,0:T(8,128)(2,1)} %tmpl.1), custom_call_target="tpu_custom_call" | custom-call | tf_op jit(solution)/shard_map/iteration/pallas_call | solution.py:457
  72.2 3.5 %widen.1 = (f32[3200,128]{1,0:T(8,128)}, f32[1,128]{1,0:T(1,128)}) custom-call(bf16[3200,128]{1,0:T(8,128)(2,1)} %get-tuple-element.6.means, f32[1,128]{1,0:T(1,128)} %get-tuple-element.7.loglik), custom_call_target="tpu_custom_call" | custom-call | tf_op jit(solution)/shard_map/widen/pallas_call | solution.py:500

commit v6 on v5

--- a/solution.py
+++ b/solution.py
@@ -166,7 +166,7 @@
             flat[pl.ds(pl.multiple_of((i * slots + j) * (BOX // 2), BOX // 2), BOX // 2), :] = jnp.where(lanes < BOX, e, o)
             return 0
 
-        lax.fori_loop(0, slots, cut, 0, unroll=8)
+        lax.fori_loop(0, slots, cut, 0, unroll=16)
 
     for s in range(BOX // 2):
         boxes[:, s * ANG : (s + 1) * ANG] = flat[pl.ds(s, parts, stride=BOX // 2), :].astype(BF16)
@@ -203,11 +203,11 @@
                     part = pltpu.roll(whole, turn, 1) if turn else whole
                     shifted[j * parts : (j + 1) * parts, c0 : c0 + ANG] = part.astype(BF16)
 
-    rows = lax.broadcasted_iota(jnp.int32, (NROWS, 1), 0)
+    spare = [2 * CPAD * k + 8 * h + 196 for k in range(4) for h in range(2)]
+    for start in spare:
+        esum[start : start + 4, :] = jnp.full((4, ANG), 1e28, F32)
+    esum[NROWS - 12 :, :] = jnp.full((12, ANG), 1e28, F32)
     energy = 0.5 * jnp.sum(esum[...], axis=1, keepdims=True)
-    paired = lax.rem(rows >> 4, 13) * 8 + (rows & 7)
-    pad = jnp.where(rows < 8 * CPAD, paired, rows - 8 * CPAD) >= CLASSES
-    energy = jnp.where(pad, 1e30, energy)
 
     def score(j, peak):
         rows_j = pl.ds(pl.multiple_of(j * parts, parts), parts)
@@ -496,10 +496,10 @@
 
 
 def widen(means, loglik):
-    rows = CLASSES * RAD // 4
+    rows = CLASSES * RAD // 2
     return pl.pallas_call(
         widen_kernel,
-        grid=(4,),
+        grid=(2,),
         out_shape=(
             jax.ShapeDtypeStruct((CLASSES * RAD, ANG), F32),
             jax.ShapeDtypeStruct((1, ANG), F32),

time: 75.8 us -> 73.3 us (0.967)
  Pallas kernels: 75 us -> 72.5 us
    pallas_call x1, Pallas kernels: 71.5 us -> 70.2 us  [iteration(): pl.pallas_call(iteration_kernel, out_shape=(jax.ShapeDtypeStruct((CLASSES...]
    pallas_call x1, Pallas kernels: 3.46 us -> 2.24 us  [widen(): pl.pallas_call(widen_kernel, grid=(2,), out_shape=(jax.ShapeDtypeStruct((...]
where the time goes in v6:
time: 73.3 us; the launch traced here: 73.1 us
  Pallas kernels  72.5 us (99%)
    pallas_call x1, Pallas kernels, iteration(): pl.pallas_call(iteration_kernel, out_shape=(jax.ShapeDtypeStruct((CLASSES...  70.2 us
    pallas_call x1, Pallas kernels, widen(): pl.pallas_call(widen_kernel, grid=(2,), out_shape=(jax.ShapeDtypeStruct((...  2.24 us

profile of v6, /device:TPU:1, one launch (start us, length us, event | category | flops | bytes accessed | tf_op | source)
XLA Modules:
  0.0 73.1 jit_solution(15816728316205477689)
XLA Ops:
  0.6 70.2 %iteration.1 = (bf16[3200,128]{1,0:T(8,128)(2,1)}, f32[1,128]{1,0:T(1,128)}) custom-call(s32[2,4,64]{2,1,0:T(4,128)} %pos.1, s32[4]{0:T(128)} %counts.1, bf16[4,1024,1024]{2,1,0:T(8,128)(2,1)} %mic.1, s32[4,64]{1,0:T(4,128)} %dest.1, f32[1,4096]{1,0:T(1,128)} %constant.4.clone.ys, f32[1,4096]{1,0:T(1,128)} %constant.5.clone.xs, bf16[100,32,128]{2,1,0:T(8,128)(2,1)} %tmpl.1), custom_call_target="tpu_custom_call" | custom-call | tf_op jit(solution)/shard_map/iteration/pallas_call | solution.py:457
  70.9 2.2 %widen.1 = (f32[3200,128]{1,0:T(8,128)}, f32[1,128]{1,0:T(1,128)}) custom-call(bf16[3200,128]{1,0:T(8,128)(2,1)} %get-tuple-element.6.means, f32[1,128]{1,0:T(1,128)} %get-tuple-element.7.loglik), custom_call_target="tpu_custom_call" | custom-call | tf_op jit(solution)/shard_map/widen/pallas_call | solution.py:500

commit v7 on v6

--- a/solution.py
+++ b/solution.py
@@ -119,7 +119,7 @@
     lax.fori_loop(0, RAD // 2, regroup, 0, unroll=2)
 
     def rotate_block(n, _):
-        few = 4
+        few = 8
         block = byrad[pl.ds(pl.multiple_of(n * few * CPAD, 16), few * CPAD), :]
         for k in range(5):
             start, height = (k * 2 * CPAD, 2 * CPAD) if k < 4 else (8 * CPAD, 112)
@@ -140,7 +140,7 @@
             esum[start : start + height, :] += total
         return 0
 
-    lax.fori_loop(0, RAD // 4, rotate_block, 0)
+    lax.fori_loop(0, RAD // 8, rotate_block, 0)
 
     lanes = lax.broadcasted_iota(jnp.int32, (BOX // 2, ANG), 1)
     for i in range(mics):
@@ -166,7 +166,7 @@
             flat[pl.ds(pl.multiple_of((i * slots + j) * (BOX // 2), BOX // 2), BOX // 2), :] = jnp.where(lanes < BOX, e, o)
             return 0
 
-        lax.fori_loop(0, slots, cut, 0, unroll=16)
+        lax.fori_loop(0, slots, cut, 0, unroll=32)
 
     for s in range(BOX // 2):
         boxes[:, s * ANG : (s + 1) * ANG] = flat[pl.ds(s, parts, stride=BOX // 2), :].astype(BF16)

time: 73.3 us -> 72.1 us (0.984)
  Pallas kernels: 72.5 us -> 71.3 us
    pallas_call x1, Pallas kernels: 70.2 us -> 69.1 us  [iteration(): pl.pallas_call(iteration_kernel, out_shape=(jax.ShapeDtypeStruct((CLASSES...]
where the time goes in v7:
time: 72.1 us; the launch traced here: 71.9 us
  Pallas kernels  71.3 us (99%)
    pallas_call x1, Pallas kernels, iteration(): pl.pallas_call(iteration_kernel, out_shape=(jax.ShapeDtypeStruct((CLASSES...  69.1 us
    pallas_call x1, Pallas kernels, widen(): pl.pallas_call(widen_kernel, grid=(2,), out_shape=(jax.ShapeDtypeStruct((...  2.24 us

profile of v7, /device:TPU:1, one launch (start us, length us, event | category | flops | bytes accessed | tf_op | source)
XLA Modules:
  0.0 71.9 jit_solution(13149474959215027970)
XLA Ops:
  0.6 69.1 %iteration.1 = (bf16[3200,128]{1,0:T(8,128)(2,1)}, f32[1,128]{1,0:T(1,128)}) custom-call(s32[2,4,64]{2,1,0:T(4,128)} %pos.1, s32[4]{0:T(128)} %counts.1, bf16[4,1024,1024]{2,1,0:T(8,128)(2,1)} %mic.1, s32[4,64]{1,0:T(4,128)} %dest.1, f32[1,4096]{1,0:T(1,128)} %constant.4.clone.ys, f32[1,4096]{1,0:T(1,128)} %constant.5.clone.xs, bf16[100,32,128]{2,1,0:T(8,128)(2,1)} %tmpl.1), custom_call_target="tpu_custom_call" | custom-call | tf_op jit(solution)/shard_map/iteration/pallas_call | solution.py:457
  69.7 2.2 %widen.1 = (f32[3200,128]{1,0:T(8,128)}, f32[1,128]{1,0:T(1,128)}) custom-call(bf16[3200,128]{1,0:T(8,128)(2,1)} %get-tuple-element.6.means, f32[1,128]{1,0:T(1,128)} %get-tuple-element.7.loglik), custom_call_target="tpu_custom_call" | custom-call | tf_op jit(solution)/shard_map/widen/pallas_call | solution.py:500
